TPU v7x, 32 devices: a whole 2x2x4 slice. The times are simulated.
32 devices in a mesh: dp: 8 (over y, x, core), tensor: 4 (over z).
Axes of the slice: x: 2, y: 2, z: 4, core: 2. Of those that a mesh axis runs over, the one named last changes fastest.
Arguments:
- inputs: float32 [4096, 768], P(('dp', 'tensor')), may hold values from -6 to 6
- lengths: int32 [8], P('dp'), may hold values from 64 to 512, as said below
- qkv_weight: bfloat16 [1, 3, 768, 768], P(None, None, 'dp', 'tensor'), may hold values from -0.21875 to 0.21875
- qv_bias: float32 [1, 2, 768], P(None, None, 'tensor'), may hold values from -3 to 3
- proj_weight: bfloat16 [1, 768, 768], P(None, 'tensor', 'dp'), may hold values from -1.75 to 1.75
- branch_bias: float32 [1, 2, 768], replicated, may hold values from -3 to 3
- up_weight: bfloat16 [1, 768, 3072], P(None, 'dp', 'tensor'), may hold values from -0.21875 to 0.21875
- up_bias: float32 [1, 3072], P(None, 'tensor'), may hold values from -3 to 3
- down_weight: bfloat16 [1, 3072, 768], P(None, 'tensor', 'dp'), may hold values from -0.109375 to 0.109375
- norm_gain: float32 [1, 2, 768], replicated, may hold values from 0.5 to 1.5
- norm_bias: float32 [1, 2, 768], replicated, may hold values from -3 to 3
- cotangent: float32 [4096, 768], P(('dp', 'tensor')), may hold values from -6 to 6
Outputs:
- outputs: float32 [4096, 768], P(('dp', 'tensor'))
- input_grad: float32 [4096, 768], P(('dp', 'tensor'))
- qkv_grad: float32 [1, 3, 768, 768], P(None, None, 'dp', 'tensor')
- qvbias_grad: float32 [1, 2, 768], P(None, None, 'tensor')
- proj_grad: float32 [1, 768, 768], P(None, 'tensor', 'dp')
- branch_grad: float32 [1, 2, 768], replicated
- up_grad: float32 [1, 768, 3072], P(None, 'dp', 'tensor')
- upbias_grad: float32 [1, 3072], P(None, 'tensor')
- down_grad: float32 [1, 3072, 768], P(None, 'tensor', 'dp')
- gain_grad: float32 [1, 2, 768], replicated
- normbias_grad: float32 [1, 2, 768], replicated
Inputs may be any that keep to these rules, and one draw needn't show every extreme that they name: `lengths`: every draw has a sequence with all 512 tokens valid.
All inputs are finite; a program needn't handle non-finite values.
Results may differ from a plain program's by a relative error of at most 0.019.
Values may be sent and summed in bfloat16 or wider, within the bound.
A program may use at most 64 MiB of HBM per device.

v0:
```python
import math

import jax
import jax.numpy as jnp
from jax import lax
from jax.sharding import PartitionSpec as P

HD = 64
L = 512
LAYERS = 1


norm_eps = 1e-12
half_root = 0.7071067811865476
inv_root = 0.3989422804014327


def layer_norm(residual):
    centred = residual - jnp.mean(residual, axis=-1, keepdims=True)
    inverse = lax.rsqrt(jnp.mean(centred * centred, axis=-1, keepdims=True) + norm_eps)
    return (centred * inverse, inverse)


def norm_back(upstream, normed, inverse, gain_row):
    scaled = upstream * gain_row
    return inverse * (
        scaled
        - jnp.mean(scaled, axis=-1, keepdims=True)
        - normed * jnp.mean(scaled * normed, axis=-1, keepdims=True)
    )


def gelu_value(pre_act):
    return 0.5 * pre_act * (1.0 + lax.erf(pre_act * half_root))


def gelu_slope(pre_act):
    return (
        0.5 * (1.0 + lax.erf(pre_act * half_root))
        + pre_act * jnp.exp(-0.5 * pre_act * pre_act) * inv_root
    )


def score_block(queries, key_rows, key_valid):
    raw_scores = jnp.einsum(
        "sqhc,skhc->shqk", queries, key_rows, preferred_element_type=jnp.float32
    ) * (1.0 / math.sqrt(HD))
    return jnp.where(key_valid[:, None, None, :], raw_scores, -1e30)


def fetch_weights(qkv_weight, proj_weight, up_weight, down_weight, layer_index):
    return (
        lax.all_gather(qkv_weight[layer_index], "dp", axis=1, tiled=True),
        lax.all_gather(proj_weight[layer_index], "dp", axis=1, tiled=True),
        lax.all_gather(up_weight[layer_index], "dp", axis=0, tiled=True),
        lax.all_gather(down_weight[layer_index], "dp", axis=1, tiled=True),
    )


def gather_rows(block_rows):
    return lax.all_gather(block_rows, "tensor", axis=0, tiled=True)


def gather_grads(block_rows):
    return lax.all_gather(block_rows, "tensor", axis=0, tiled=True)


def scatter_rows(left_rows, weight):
    return lax.psum_scatter(
        jnp.dot(left_rows, weight, preferred_element_type=jnp.float32).astype(jnp.bfloat16),
        "tensor",
        scatter_dimension=0,
        tiled=True,
    ).astype(jnp.float32)


def scatter_back(term_rows, own_rows):
    return lax.psum_scatter(
        term_rows(jnp.int32(0), own_rows * lax.axis_size("tensor")).astype(jnp.bfloat16),
        "tensor",
        scatter_dimension=0,
        tiled=True,
    ).astype(jnp.float32)


def per_device(
    inputs,
    lengths,
    qkv_weight,
    qv_bias,
    proj_weight,
    branch_bias,
    up_weight,
    up_bias,
    down_weight,
    norm_gain,
    norm_bias,
    cotangent,
):
    own_rows = inputs.shape[0]
    seq_count = lengths.shape[0]
    head_count = qkv_weight.shape[3] // HD
    head_shape = (seq_count, L, head_count, HD)
    key_valid = jnp.arange(L, dtype=jnp.int32)[None, :] < lengths[:, None]
    hidden = inputs
    layer_index = 0
    weights_now = fetch_weights(qkv_weight, proj_weight, up_weight, down_weight, layer_index)
    qkv_full, proj_full, up_full, down_full = weights_now
    rounded = gather_rows(hidden.astype(jnp.bfloat16))
    total_rows = rounded.shape[0]
    mixed_rows = jnp.einsum("rd,jde->jre", rounded, qkv_full, preferred_element_type=jnp.float32)
    queries = (mixed_rows[0] + qv_bias[layer_index, 0]).astype(jnp.bfloat16).reshape(head_shape)
    key_rows = mixed_rows[1].astype(jnp.bfloat16).reshape(head_shape)
    values = (mixed_rows[2] + qv_bias[layer_index, 1]).astype(jnp.bfloat16).reshape(head_shape)
    scores = score_block(queries, key_rows, key_valid)
    row_peak = jnp.max(scores, axis=-1, keepdims=True)
    log_total = row_peak + jnp.log(jnp.sum(jnp.exp(scores - row_peak), axis=-1, keepdims=True))
    soft_weights = jnp.exp(scores - log_total).astype(jnp.bfloat16)
    context = (
        jnp.einsum("shqk,skhc->sqhc", soft_weights, values, preferred_element_type=jnp.float32)
        .astype(jnp.bfloat16)
        .reshape(total_rows, head_count * HD)
    )
    residual = hidden + scatter_rows(context, proj_full) + branch_bias[layer_index, 0]
    normed_one, inverse_one = layer_norm(residual)
    middle = normed_one * norm_gain[layer_index, 0] + norm_bias[layer_index, 0]
    middle_rows = gather_rows(middle.astype(jnp.bfloat16))
    pre_act = (
        jnp.dot(middle_rows, up_full, preferred_element_type=jnp.float32) + up_bias[layer_index]
    )
    active = gelu_value(pre_act).astype(jnp.bfloat16)
    residual_two = middle + scatter_rows(active, down_full) + branch_bias[layer_index, 1]
    normed_two, inverse_two = layer_norm(residual_two)
    stored = [
        (
            rounded,
            queries,
            key_rows,
            values,
            log_total,
            context,
            normed_one,
            inverse_one,
            middle_rows,
            pre_act,
            active,
            normed_two,
            inverse_two,
        )
    ]
    hidden = normed_two * norm_gain[layer_index, 1] + norm_bias[layer_index, 1]
    big_grads = [None] * LAYERS
    qvbias_parts = [None] * LAYERS
    upbias_parts = [None] * LAYERS
    branch_parts = [None] * LAYERS
    gain_parts = [None] * LAYERS
    nbias_parts = [None] * LAYERS
    upstream = cotangent
    for layer_index in reversed(range(LAYERS)):
        (
            rounded,
            queries,
            key_rows,
            values,
            log_total,
            context,
            normed_one,
            inverse_one,
            middle_rows,
            pre_act,
            active,
            normed_two,
            inverse_two,
        ) = stored[layer_index]
        qkv_full, proj_full, up_full, down_full = fetch_weights(
            qkv_weight, proj_weight, up_weight, down_weight, layer_index
        )
        total_rows = rounded.shape[0]
        gain_two = jnp.sum(upstream * normed_two, axis=0)
        nbias_two = jnp.sum(upstream, axis=0)
        dres_two = norm_back(upstream, normed_two, inverse_two, norm_gain[layer_index, 1])
        branch_two = jnp.sum(dres_two, axis=0)
        dres_two_all = gather_grads(dres_two.astype(jnp.bfloat16))
        down_part = jnp.einsum(
            "rf,rd->fd", active, dres_two_all, preferred_element_type=jnp.float32
        )
        dpre = jnp.einsum(
            "rd,fd->rf", dres_two_all, down_full, preferred_element_type=jnp.float32
        ) * gelu_slope(pre_act)
        upbias_parts[layer_index] = jnp.sum(dpre, axis=0)
        dpre_b = dpre.astype(jnp.bfloat16)
        up_part = jnp.einsum("rd,rf->df", middle_rows, dpre_b, preferred_element_type=jnp.float32)

        def unit_rows(row_start, row_count):
            return jnp.einsum("rf,df->rd", dpre_b, up_full, preferred_element_type=jnp.float32)

        dmiddle = dres_two + scatter_back(unit_rows, own_rows)
        gain_one = jnp.sum(dmiddle * normed_one, axis=0)
        nbias_one = jnp.sum(dmiddle, axis=0)
        dres_one = norm_back(dmiddle, normed_one, inverse_one, norm_gain[layer_index, 0])
        branch_one = jnp.sum(dres_one, axis=0)
        dres_one_all = gather_grads(dres_one.astype(jnp.bfloat16))
        proj_part = jnp.einsum(
            "rc,rd->cd", context, dres_one_all, preferred_element_type=jnp.float32
        )
        dcontext = (
            jnp.einsum("rd,cd->rc", dres_one_all, proj_full, preferred_element_type=jnp.float32)
            .astype(jnp.bfloat16)
            .reshape(head_shape)
        )
        scores = score_block(queries, key_rows, key_valid)
        probs_full = jnp.exp(scores - log_total)
        dprob = jnp.einsum("sqhc,skhc->shqk", dcontext, values, preferred_element_type=jnp.float32)
        dscore = (
            probs_full
            * (dprob - jnp.sum(probs_full * dprob, axis=-1, keepdims=True))
            * (1.0 / math.sqrt(HD))
        ).astype(jnp.bfloat16)
        dquery = jnp.einsum("shqk,skhc->sqhc", dscore, key_rows, preferred_element_type=jnp.float32)
        dkey = jnp.einsum("shqk,sqhc->skhc", dscore, queries, preferred_element_type=jnp.float32)
        dvalue = jnp.einsum(
            "shqk,sqhc->skhc",
            probs_full.astype(jnp.bfloat16),
            dcontext,
            preferred_element_type=jnp.float32,
        )
        dmixed_full = jnp.stack([dquery, dkey, dvalue]).reshape(3, total_rows, head_count * HD)
        qvbias_parts[layer_index] = jnp.stack(
            [jnp.sum(dmixed_full[0], axis=0), jnp.sum(dmixed_full[2], axis=0)]
        )
        dmixed = dmixed_full.astype(jnp.bfloat16)
        qkv_part = jnp.einsum("rd,jre->jde", rounded, dmixed, preferred_element_type=jnp.float32)

        def head_rows(row_start, row_count):
            return jnp.einsum("jre,jde->rd", dmixed, qkv_full, preferred_element_type=jnp.float32)

        upstream = dres_one + scatter_back(head_rows, own_rows)
        branch_parts[layer_index] = jnp.stack([branch_one, branch_two])
        gain_parts[layer_index] = jnp.stack([gain_one, gain_two])
        nbias_parts[layer_index] = jnp.stack([nbias_one, nbias_two])
        big_grads[layer_index] = (
            lax.psum_scatter(qkv_part, "dp", scatter_dimension=1, tiled=True),
            lax.psum_scatter(proj_part, "dp", scatter_dimension=1, tiled=True),
            lax.psum_scatter(up_part, "dp", scatter_dimension=0, tiled=True),
            lax.psum_scatter(down_part, "dp", scatter_dimension=1, tiled=True),
        )
    qkv_out = jnp.stack([layer_entry[0] for layer_entry in big_grads])
    proj_out = jnp.stack([layer_entry[1] for layer_entry in big_grads])
    up_out = jnp.stack([layer_entry[2] for layer_entry in big_grads])
    down_out = jnp.stack([layer_entry[3] for layer_entry in big_grads])
    qvbias_out, upbias_out = lax.psum((jnp.stack(qvbias_parts), jnp.stack(upbias_parts)), "dp")
    branch_out, gain_out, normbias_out = lax.psum(
        (jnp.stack(branch_parts), jnp.stack(gain_parts), jnp.stack(nbias_parts)), ("dp", "tensor")
    )
    return (
        hidden,
        upstream,
        qkv_out,
        qvbias_out,
        proj_out,
        branch_out,
        up_out,
        upbias_out,
        down_out,
        gain_out,
        normbias_out,
    )


def solution(mesh):
    placed = (
        P(("dp", "tensor"), None),
        P("dp"),
        P(None, None, "dp", "tensor"),
        P(None, None, "tensor"),
        P(None, "tensor", "dp"),
        P(),
        P(None, "dp", "tensor"),
        P(None, "tensor"),
        P(None, "tensor", "dp"),
        P(),
        P(),
        P(("dp", "tensor"), None),
    )
    return jax.shard_map(
        per_device,
        mesh=mesh,
        in_specs=placed,
        out_specs=(
            P(("dp", "tensor"), None),
            P(("dp", "tensor"), None),
            P(None, None, "dp", "tensor"),
            P(None, None, "tensor"),
            P(None, "tensor", "dp"),
            P(),
            P(None, "dp", "tensor"),
            P(None, "tensor"),
            P(None, "tensor", "dp"),
            P(),
            P(),
        ),
        check_vma=False,
    )
```

profile of v0, /device:TPU:0, one launch (start us, length us, event | category | flops | bytes accessed | tf_op | source)
XLA Modules:
  0.0 422.3 jit_solution(15051077807394162095)
XLA Ops:
  10.1 21.7 %all_gather.29 = bf16[512,768]{1,0:T(8,128)(2,1)} all-gather(bf16[128,768]{1,0:T(8,128)(2,1)S(1)} %convert_element_type.83), channel_id=1, replica_groups=mesh['dp'=8,'tensor'=4] {'tensor'}, dimensions={0}, use_global_device_ids=true | all-gather | bytes 983040 | tf_op jit(solution)/shard_map/all_gather | solution.py:61
  31.8 13.2 %all-gather = bf16[1,3,768,192]{3,1,0,2:T(4,128)(2,1)S(1)} all-gather(bf16[1,3,96,192]{3,1,0,2:T(4,128)(2,1)S(1)} %copy.37), channel_id=2, replica_groups=mesh['dp'=8,'tensor'=4] {'dp'}, dimensions={2}, use_global_device_ids=true | all-gather | bytes 995328 | tf_op jit(solution)/shard_map/all_gather | solution.py:53
  45.9 2.1 convolution_bitcast_fusion.1
  50.7 9.3 %all-gather.1 = bf16[1,192,768]{1,0,2:T(2,128)(2,1)S(1)} all-gather(bf16[1,192,96]{1,0,2:T(2,128)(2,1)S(1)} %copy.40), channel_id=3, replica_groups=mesh['dp'=8,'tensor'=4] {'dp'}, dimensions={2}, use_global_device_ids=true | all-gather | bytes 331776 | tf_op jit(solution)/shard_map/all_gather | solution.py:54
  60.4 2.1 fusion.4
  68.7 19.9 %reduce-scatter.13.cloned.1.call-done = bf16[128,768]{1,0:T(8,128)(2,1)} async-done(((bf16[512,768]{1,0:T(8,128)(2,1)}), bf16[128,768]{1,0:T(8,128)(2,1)}) %reduce-scatter.13.cloned.1.call-update) | async-done | bytes 196624 | tf_op jit(solution)/shard_map/reduce_scatter | solution.py:69
  90.6 18.4 %all_gather.31 = bf16[512,768]{1,0:T(8,128)(2,1)} all-gather(bf16[128,768]{1,0:T(8,128)(2,1)S(1)} %fusion.37), channel_id=1, replica_groups=mesh['dp'=8,'tensor'=4] {'tensor'}, dimensions={0}, use_global_device_ids=true | all-gather | bytes 983040 | tf_op jit(solution)/shard_map/all_gather | solution.py:61
  108.9 3.8 multiply_convert_fusion.1
  112.7 4.3 %all-gather.9.cloned.1.call-done = bf16[1,768,768]{1,2,0:T(8,128)(2,1)} async-done(((bf16[1,768,96]{1,2,0:T(8,128)(2,1)}), bf16[1,768,768]{1,2,0:T(8,128)(2,1)}) %all-gather.9.cloned.1.call-update) | async-done | bytes 1179664 | tf_op jit(solution)/shard_map/all_gather | solution.py:56
  117.0 3.2 convolution_convert_fusion.1
  120.3 23.4 %reduce-scatter.15.cloned.1.call-done = bf16[128,768]{1,0:T(8,128)(2,1)} async-done(((bf16[512,768]{1,0:T(8,128)(2,1)}), bf16[128,768]{1,0:T(8,128)(2,1)}) %reduce-scatter.15.cloned.1.call-update) | async-done | bytes 196624 | tf_op jit(solution)/shard_map/reduce_scatter | solution.py:69
  145.3 1.8 multiply_reduce_fusion.1
  147.1 2.1 fusion.50
  149.2 18.0 %all_gather.34 = bf16[512,768]{1,0:T(8,128)(2,1)S(1)} all-gather(bf16[128,768]{1,0:T(8,128)(2,1)S(1)} %get-tuple-element.68), channel_id=1, replica_groups=mesh['dp'=8,'tensor'=4] {'tensor'}, dimensions={0}, use_global_device_ids=true | all-gather | bytes 983040 | tf_op jit(solution)/shard_map/all_gather | solution.py:65
  171.6 22.7 %reduce-scatter.17.cloned.1.call-done = bf16[128,768]{1,0:T(8,128)(2,1)} async-done(((bf16[512,768]{1,0:T(8,128)(2,1)}), bf16[128,768]{1,0:T(8,128)(2,1)}) %reduce-scatter.17.cloned.1.call-update) | async-done | bytes 196624 | tf_op jit(solution)/shard_map/reduce_scatter | solution.py:78
  194.3 2.0 multiply_reduce_fusion.2
  196.2 1.8 fusion.49
  198.8 18.0 %all_gather.35 = bf16[512,768]{1,0:T(8,128)(2,1)S(1)} all-gather(bf16[128,768]{1,0:T(8,128)(2,1)S(1)} %convert_element_type.101), channel_id=1, replica_groups=mesh['dp'=8,'tensor'=4] {'tensor'}, dimensions={0}, use_global_device_ids=true | all-gather | bytes 983040 | tf_op jit(solution)/shard_map/all_gather | solution.py:65
  219.6 3.4 fusion.40
  222.9 6.2 %fusion.54 = (f32[3,64]{1,0:T(4,128)}, bf16[1,512,3,64]{1,3,2,0:T(8,128)(2,1)}) fusion(bf16[512,3,64]{0,2,1:T(8,128)(2,1)} %bitcast.107, f32[3,512,512]{1,2,0:T(8,128)} %fusion.40, f32[3,512]{1,0:T(4,128)} %copy-done.26, f32[3,512,512]{1,2,0:T(8,128)S(1)} %get-tuple-element.82, pred[512]{0:T(512)(128)(4,1)} %copy-done.34), kind=kOutput, calls=%fused_computation.108 | convolution fusion | flops 109512512 | bytes 6692096 | tf_op jit(solution)/shard_map/shqk,skhc->sqhc/dot_general | solution.py:219
  229.1 5.5 %fusion.25 = bf16[3,64,512]{2,1,0:T(8,128)(2,1)} fusion(f32[3,512,512]{1,2,0:T(8,128)} %fusion.40, f32[512,3,64]{0,2,1:T(8,128)S(1)} %bitcast.100, f32[3,64]{1,0:T(4,128)S(1)} %copy-done.22, f32[3,512,512]{1,2,0:T(8,128)S(1)} %get-tuple-element.82, f32[3,512]{1,0:T(4,128)} %copy-done.26, pred[512]{0:T(512)(128)(4,1)} %copy-done.34), kind=kOutput, calls=%fused_computation.34 | convolution fusion | flops 109611008 | bytes 6888704 | tf_op jit(solution)/shard_map/shqk,sqhc->skhc/dot_general | solution.py:220
  234.7 2.0 fusion.55
  239.2 2.8 convolution_bitcast_fusion
  242.0 3.0 copy.50
  245.0 2.8 reshape.208
  247.9 3.7 fusion.59
  251.8 2.2 fusion.34
  254.3 12.7 %all-reduce.1 = (f32[1,2,192]{2,1,0:T(2,128)}, f32[1,768]{1,0:T(1,128)}) all-reduce(f32[1,2,192]{2,1,0:T(2,128)S(1)} %maximum_bitcast_fusion.3, f32[1,768]{1,0:T(1,128)S(1)} %stack.90), channel_id=1, replica_groups=mesh['dp'=8,'tensor'=4] {'dp'}, use_global_device_ids=true, to_apply=%region_18.19 | all-reduce | flops 1152 | bytes 9216 | tf_op jit(solution)/shard_map/psum | solution.py:251
  267.0 38.2 %all-reduce = (f32[1,2,768]{2,1,0:T(2,128)}, f32[1,2,768]{2,1,0:T(2,128)}, f32[1,2,768]{2,1,0:T(2,128)}) all-reduce(f32[1,2,768]{2,1,0:T(2,128)S(1)} %maximum_bitcast_fusion, f32[1,2,768]{2,1,0:T(2,128)S(1)} %maximum_bitcast_fusion.1, f32[1,2,768]{2,1,0:T(2,128)S(1)} %maximum_bitcast_fusion.2), channel_id=1, replica_groups=mesh['dp'=8,'tensor'=4] {'dp','tensor'}, use_global_device_ids=true, to_apply=%region_22.23 | all-reduce | flops 4608 | bytes 36864 | tf_op jit(solution)/shard_map/psum | solution.py:252
  308.6 13.8 %reduce-scatter.25.cloned.1.call-done = f32[96,576]{1,0:T(8,128)} async-done(((f32[768,576]{1,0:T(8,128)}), f32[96,576]{1,0:T(8,128)}) %reduce-scatter.25.cloned.1.call-update) | async-done | bytes 221200
  324.3 44.8 %reduce-scatter.23.cloned.1.call-done = f32[768,96]{0,1:T(8,128)} async-done(((f32[768,768]{0,1:T(8,128)}), f32[768,96]{0,1:T(8,128)}) %reduce-scatter.23.cloned.1.call-update) | async-done | bytes 294928 | tf_op jit(solution)/shard_map/reduce_scatter | solution.py:245
  369.0 46.1 %reduce-scatter.21.cloned.1.call-done = f32[96,768]{1,0:T(8,128)} async-done(((f32[768,768]{1,0:T(8,128)}), f32[96,768]{1,0:T(8,128)}) %reduce-scatter.21.cloned.1.call-update) | async-done | bytes 294928 | tf_op jit(solution)/shard_map/reduce_scatter | solution.py:244
  (161 shorter events, 30.9 us)
Async XLA Ops:
  8.0 80.6 %reduce-scatter.13.cloned.1.call-start = ((), (), s32[]{:S(2)}) async-start(), calls=%async_computation.8 | async-start | bytes 983040 | tf_op jit(solution)/shard_map/reduce_scatter | solution.py:69
  45.0 5.3 %copy-start.33 = (f32[1,2,192]{2,1,0:T(2,128)S(1)}, f32[1,2,192]{2,1,0:T(2,128)}, u32[]{:S(2)}) copy-start(f32[1,2,192]{2,1,0:T(2,128)} %param.15) | copy-start | bytes 4612
  45.0 5.5 %copy-start.16 = (bf16[1,192,96]{2,1,0:T(8,128)(2,1)S(1)}, bf16[1,192,96]{2,1,0:T(8,128)(2,1)}, u32[]{:S(2)}) copy-start(bf16[1,192,96]{2,1,0:T(8,128)(2,1)} %param.16) | copy-start | bytes 110596
  45.9 14.5 %copy-start.1 = (bf16[1,3,768,192]{2,3,1,0:T(8,128)(2,1)}, bf16[1,3,768,192]{2,3,1,0:T(8,128)(2,1)S(1)}, u32[]{:S(2)}) copy-start(bf16[1,3,768,192]{2,3,1,0:T(8,128)(2,1)S(1)} %copy.38) | copy-start | bytes 2654212
  50.3 12.9 %copy-start.34 = (pred[512]{0:T(512)(128)(4,1)}, pred[512]{0:T(512)(128)(4,1)S(1)}, u32[]{:S(2)}) copy-start(pred[512]{0:T(512)(128)(4,1)S(1)} %iota_compare_fusion) | copy-start | bytes 1540
  50.4 12.8 %copy-start.21 = (f32[3,64]{1,0:T(4,128)}, f32[3,64]{1,0:T(4,128)S(1)}, u32[]{:S(2)}) copy-start(f32[3,64]{1,0:T(4,128)S(1)} %add.148) | copy-start | bytes 2308
  50.5 12.7 %copy-start.24 = (f32[3,64]{1,0:T(4,128)}, f32[3,64]{1,0:T(4,128)S(1)}, u32[]{:S(2)}) copy-start(f32[3,64]{1,0:T(4,128)S(1)} %add.145) | copy-start | bytes 2308
  60.4 3.8 copy-start.7
  63.3 4.1 copy-start.31
  63.3 4.7 %copy-start.27 = (f32[1,2,768]{2,1,0:T(2,128)S(1)}, f32[1,2,768]{2,1,0:T(2,128)}, u32[]{:S(2)}) copy-start(f32[1,2,768]{2,1,0:T(2,128)} %param.17) | copy-start | bytes 18436
  63.3 5.4 %copy-start.28 = (f32[1,2,768]{2,1,0:T(2,128)S(1)}, f32[1,2,768]{2,1,0:T(2,128)}, u32[]{:S(2)}) copy-start(f32[1,2,768]{2,1,0:T(2,128)} %param.21) | copy-start | bytes 18436
  63.3 5.4 %copy-start.29 = (f32[1,2,768]{2,1,0:T(2,128)S(1)}, f32[1,2,768]{2,1,0:T(2,128)}, u32[]{:S(2)}) copy-start(f32[1,2,768]{2,1,0:T(2,128)} %param.22) | copy-start | bytes 18436
  66.2 42.7 %all-gather.7.cloned.1.call-start = ((), (), s32[]{:S(2)}) async-start(), calls=%async_computation.14 | async-start | bytes 1327104 | tf_op jit(solution)/shard_map/all_gather | solution.py:55
  66.8 50.3 %all-gather.9.cloned.1.call-start = ((), (), s32[]{:S(2)}) async-start(), calls=%async_computation.15 | async-start | bytes 1327104 | tf_op jit(solution)/shard_map/all_gather | solution.py:56
  67.4 76.4 %reduce-scatter.15.cloned.1.call-start = ((), (), s32[]{:S(2)}) async-start(), calls=%async_computation.9 | async-start | bytes 983040 | tf_op jit(solution)/shard_map/reduce_scatter | solution.py:69
  120.3 74.0 %reduce-scatter.17.cloned.1.call-start = ((), (), s32[]{:S(2)}) async-start(), calls=%async_computation.10 | async-start | bytes 983040 | tf_op jit(solution)/shard_map/reduce_scatter | solution.py:78
  143.7 23.5 %copy-start.36 = (bf16[1,768,768]{1,2,0:T(8,128)(2,1)S(1)}, bf16[1,768,768]{1,2,0:T(8,128)(2,1)}, u32[]{:S(2)}) copy-start(bf16[1,768,768]{1,2,0:T(8,128)(2,1)} %all-gather.9.cloned.1.call-done) | copy-start | bytes 3538948
  143.7 23.5 %copy-start.41 = (f32[512,768]{1,0:T(8,128)S(1)}, f32[512,768]{1,0:T(8,128)}, u32[]{:S(2)}) copy-start(f32[512,768]{1,0:T(8,128)} %get-tuple-element.84) | copy-start | bytes 4718596
  171.5 133.7 %reduce-scatter.27.cloned.1.call-start = ((), (), s32[]{:S(2)}) async-start(), calls=%async_computation.17 | async-start | bytes 884736
  194.3 22.6 %copy-start.8 = (bf16[1,192,768]{2,1,0:T(8,128)(2,1)S(1)}, bf16[1,192,768]{2,1,0:T(8,128)(2,1)}, u32[]{:S(2)}) copy-start(bf16[1,192,768]{2,1,0:T(8,128)(2,1)} %copy-done.7) | copy-start | bytes 884740
  194.3 23.7 %copy-start.13 = (bf16[3,64,512]{2,1,0:T(8,128)(2,1)S(1)}, bf16[3,64,512]{2,1,0:T(8,128)(2,1)}, u32[]{:S(2)}) copy-start(bf16[3,64,512]{2,1,0:T(8,128)(2,1)} %copy-done.12) | copy-start | bytes 589828
  198.1 21.5 %copy-start.11 = (f32[1,512,192]{1,2,0:T(8,128)S(1)}, f32[1,512,192]{1,2,0:T(8,128)}, u32[]{:S(2)}) copy-start(f32[1,512,192]{1,2,0:T(8,128)} %get-tuple-element.75) | copy-start | bytes 1179652
  198.1 21.5 %copy-start.25 = (f32[3,64]{1,0:T(4,128)S(1)}, f32[3,64]{1,0:T(4,128)}, u32[]{:S(2)}) copy-start(f32[3,64]{1,0:T(4,128)} %copy-done.24) | copy-start | bytes 2308
  219.3 87.6 %reduce-scatter.19.cloned.1.call-start = ((), (), s32[]{:S(2)}) async-start(), calls=%async_computation.11 | async-start | bytes 983040 | tf_op jit(solution)/shard_map/reduce_scatter | solution.py:78
  222.9 6.2 %copy-start.9 = (f32[1,512,192]{1,2,0:T(8,128)S(1)}, f32[1,512,192]{1,2,0:T(8,128)}, u32[]{:S(2)}) copy-start(f32[1,512,192]{1,2,0:T(8,128)} %get-tuple-element.74) | copy-start | bytes 1179652
  222.9 6.2 %copy-start.22 = (f32[3,64]{1,0:T(4,128)S(1)}, f32[3,64]{1,0:T(4,128)}, u32[]{:S(2)}) copy-start(f32[3,64]{1,0:T(4,128)} %copy-done.21) | copy-start | bytes 2308
  239.2 83.2 %reduce-scatter.25.cloned.1.call-start = ((), (), s32[]{:S(2)}) async-start(), calls=%async_computation.16 | async-start | bytes 2211840
  247.8 3.9 copy-start
  247.8 3.9 copy-start.15
  247.8 121.2 %reduce-scatter.23.cloned.1.call-start = ((), (), s32[]{:S(2)}) async-start(), calls=%async_computation.13 | async-start | bytes 2654208 | tf_op jit(solution)/shard_map/reduce_scatter | solution.py:245
  251.7 55.2 %copy-start.4 = (f32[128,768]{1,0:T(8,128)S(1)}, f32[128,768]{1,0:T(8,128)}, u32[]{:S(2)}) copy-start(f32[128,768]{1,0:T(8,128)} %copy-done.3) | copy-start | bytes 1179652
  251.7 163.5 %reduce-scatter.21.cloned.1.call-start = ((), (), s32[]{:S(2)}) async-start(), calls=%async_computation.12 | async-start | bytes 2654208 | tf_op jit(solution)/shard_map/reduce_scatter | solution.py:244
  (20 other events, 37.4 us)
Sparse Core Ops, SparseCore 0:
  66.3 22.2 reduce-scatter.12
  120.4 23.2 reduce-scatter.14
  171.7 22.5 reduce-scatter.16
Sparse Core Ops, SparseCore 1:
  68.6 22.8 all-gather.6
  93.1 23.9 all-gather.8
  219.4 34.2 reduce-scatter.26
  256.0 23.0 reduce-scatter.18
  282.5 39.8 reduce-scatter.24
  326.7 42.3 reduce-scatter.22
  372.8 42.3 reduce-scatter.20
where the time goes:
time: 423 us; the launch traced here: 422 us
  waiting for transfers between devices  176 us (42%)
  blocking collectives  149 us (35%)
  matrix products  46.7 us (11%)
  local copies, waits for them, and re-layouts  18 us (4%)
  between operations  16.5 us (4%)
  other arithmetic  14.9 us (4%)
    reduce_scatter x1, waiting for transfers between devices, per_device(): lax.psum_scatter(up_part, 'dp', scatter_dimension=0, tiled=True)  46.1 us
    reduce_scatter x1, waiting for transfers between devices, per_device(): lax.psum_scatter(down_part, 'dp', scatter_dimension=1, tiled=True)  44.8 us
    reduce_scatter x2, waiting for transfers between devices, scatter_rows(): lax.psum_scatter(jnp.dot(left_rows, weight, preferred_element_type=jnp.fl...  43.3 us
    all_gather x2, blocking collectives, gather_rows(): return lax.all_gather(block_rows, 'tensor', axis=0, tiled=True)  40.1 us
    psum x1, blocking collectives, per_device(): lax.psum((jnp.stack(branch_parts), jnp.stack(gain_parts), jnp.stack(nbias...  38.2 us
    all_gather x2, blocking collectives, gather_grads(): return lax.all_gather(block_rows, 'tensor', axis=0, tiled=True)  36 us
    reduce_scatter x2, waiting for transfers between devices, scatter_back(): lax.psum_scatter(term_rows(jnp.int32(0), own_rows * lax.axis_size('tensor...  22.7 us
    unnamed x12, waiting for transfers between devices  15 us
  transfers between devices with their start and end apart: 10, of which 7 were waited for; matrix products, arithmetic and copies ran while one was open for 11% of the time, Pallas kernels for 0%

commit v1 on v0

v1 whole, which is shorter than its diff:
```python
import functools
import math

import jax
import jax.numpy as jnp
from jax import lax
from jax.experimental import pallas as pl
from jax.experimental.pallas import tpu as pltpu
from jax.sharding import PartitionSpec as P

MESH = pl.DeviceIdType.MESH
BF = jnp.bfloat16
F32 = jnp.float32
HD = 64
L = 512
LAYERS = 1


norm_eps = 1e-12
half_root = 0.7071067811865476
inv_root = 0.3989422804014327


def layer_norm(residual):
    centred = residual - jnp.mean(residual, axis=-1, keepdims=True)
    inverse = lax.rsqrt(jnp.mean(centred * centred, axis=-1, keepdims=True) + norm_eps)
    return (centred * inverse, inverse)


def norm_back(upstream, normed, inverse, gain_row):
    scaled = upstream * gain_row
    return inverse * (
        scaled
        - jnp.mean(scaled, axis=-1, keepdims=True)
        - normed * jnp.mean(scaled * normed, axis=-1, keepdims=True)
    )


def gelu_value(pre_act):
    return 0.5 * pre_act * (1.0 + lax.erf(pre_act * half_root))


def gelu_slope(pre_act):
    return (
        0.5 * (1.0 + lax.erf(pre_act * half_root))
        + pre_act * jnp.exp(-0.5 * pre_act * pre_act) * inv_root
    )


def score_block(queries, key_rows, key_valid):
    raw_scores = jnp.einsum(
        "sqhc,skhc->shqk", queries, key_rows, preferred_element_type=jnp.float32
    ) * (1.0 / math.sqrt(HD))
    return jnp.where(key_valid[:, None, None, :], raw_scores, -1e30)


def send(src, dst, send_sem, recv_sem, axis, target):
    return pltpu.make_async_remote_copy(
        src_ref=src,
        dst_ref=dst,
        send_sem=send_sem,
        recv_sem=recv_sem,
        device_id={axis: target},
        device_id_type=MESH,
    )


def chain_barrier(me, n, extra=0):
    barrier = pltpu.get_barrier_semaphore()

    @pl.when(me > 0)
    def _():
        pl.semaphore_signal(barrier, inc=1, device_id={"tensor": me - 1}, device_id_type=MESH)

    @pl.when(me < n - 1)
    def _():
        pl.semaphore_signal(barrier, inc=1, device_id={"tensor": me + 1}, device_id_type=MESH)

    inner = jnp.logical_and(me > 0, me < n - 1)

    @pl.when(inner)
    def _():
        pl.semaphore_wait(barrier, 2 + extra)

    @pl.when(jnp.logical_not(inner))
    def _():
        pl.semaphore_wait(barrier, 1 + extra)


def ways(me, n):
    return ((0, me, me + 1), (1, n - 1 - me, me - 1))


def chain_reduce(term, me, n, acc, tmp, sbuf, rbuf, ssem, rsem):
    def link(way, s, target):
        return send(
            sbuf.at[way, s], rbuf.at[way, s], ssem.at[way, s], rsem.at[way, s], "tensor", target
        )

    for s in range(n - 1):
        for way, pos, target in ways(me, n):
            owner = n - 1 - s + pos
            block = owner if way == 0 else n - 1 - owner

            @pl.when(pos <= s)
            def _(way=way, pos=pos, target=target, block=block):
                tmp[...] = term(block)
                if s > 0:

                    @pl.when(pos > 0)
                    def _():
                        link(way, s - 1, target).wait_recv()
                        tmp[...] += rbuf[way, s - 1].astype(F32)

                sbuf[way, s] = tmp[...].astype(BF)
                link(way, s, target).start()

    acc[...] = term(me)
    for way, pos, target in ways(me, n):

        @pl.when(pos > 0)
        def _(way=way, target=target):
            link(way, n - 2, target).wait_recv()
            acc[...] += rbuf[way, n - 2].astype(F32)

    def finish():
        for s in range(n - 1):
            for way, pos, target in ways(me, n):

                @pl.when(pos <= s)
                def _(way=way, target=target):
                    link(way, s, target).wait_send()

    return finish


def chain_gather(out, me, n, ssem, rsem, between=None):
    def link(way, s, pos, target):
        block = pos - s
        block = block if way == 0 else n - 1 - block
        return send(
            out.at[block], out.at[block], ssem.at[way, s], rsem.at[way, s], "tensor", target
        )

    for s in range(n - 1):
        for way, pos, target in ways(me, n):

            @pl.when(jnp.logical_and(pos >= s, pos < n - 1))
            def _(way=way, pos=pos, target=target):
                if s > 0:
                    link(way, s - 1, pos - 1, target).wait_recv()
                link(way, s, pos, target).start()

        if s == 0 and between is not None:
            between()
    for way, pos, target in ways(me, n):

        @pl.when(pos == n - 1)
        def _(way=way, pos=pos, target=target):
            for s in range(n - 1):
                link(way, s, pos - 1, target).wait_recv()

    for s in range(n - 1):
        for way, pos, target in ways(me, n):

            @pl.when(jnp.logical_and(pos >= s, pos < n - 1))
            def _(way=way, pos=pos, target=target):
                link(way, s, pos, target).wait_send()


def row_block(ref, block, rows):
    return ref[pl.ds(pl.multiple_of(block * rows, rows), rows), :]


def nt_dot(left, right):
    return lax.dot_general(left, right, (((1,), (1,)), ((), ())), preferred_element_type=F32)


def front_kernel(n, dp, x_ref, qkv_ref, proj_ref, rows_ref, qkv_all, proj_all, gs, gr, ws, wr):
    me = lax.axis_index("tensor")
    mine = lax.axis_index("dp")
    barrier = pltpu.get_barrier_semaphore()
    for k in range(1, dp):
        pl.semaphore_signal(
            barrier, inc=1, device_id={"dp": lax.rem(mine + k, dp)}, device_id_type=MESH
        )
    chain_barrier(me, n, dp - 1)

    def links(k):
        target = lax.rem(mine + k, dp)
        return (
            send(qkv_ref, qkv_all.at[mine], ws.at[0, k], wr.at[0, k], "dp", target),
            send(proj_ref, proj_all.at[mine], ws.at[1, k], wr.at[1, k], "dp", target),
        )

    rows_ref[me] = x_ref[...].astype(BF)

    def between():
        for k in range(1, dp):
            for copy in links(k):
                copy.start()
        qkv_all[mine] = qkv_ref[...]
        proj_all[mine] = proj_ref[...]

    chain_gather(rows_ref, me, n, gs, gr, between)
    for k in range(1, dp):
        for copy in links(k):
            copy.wait()


def attn_out_kernel(
    n, ctx, proj, hidden, bias, gain, nbias,
    normed_o, inv_o, middle_o, rows_o,
    acc, tmp, sbuf, rbuf, ss, sr, gs, gr,
):
    me = lax.axis_index("tensor")
    rows = hidden.shape[0]
    chain_barrier(me, n)
    finish = chain_reduce(
        lambda block: jnp.dot(row_block(ctx, block, rows), proj[...], preferred_element_type=F32),
        me, n, acc, tmp, sbuf, rbuf, ss, sr,
    )
    normed, inverse = layer_norm(hidden[...] + acc[...] + bias[...])
    middle = normed * gain[...] + nbias[...]
    normed_o[...] = normed
    inv_o[...] = inverse
    middle_o[...] = middle
    rows_o[me] = middle.astype(BF)
    chain_gather(rows_o, me, n, gs, gr)
    finish()


def turn_kernel(
    n, act, down, middle, bias, gain, nbias, cot,
    hidden_o, dres_o, sums_o, rows_o,
    acc, tmp, sbuf, rbuf, ss, sr, gs, gr,
):
    me = lax.axis_index("tensor")
    rows = middle.shape[0]
    chain_barrier(me, n)
    finish = chain_reduce(
        lambda block: jnp.dot(row_block(act, block, rows), down[...], preferred_element_type=F32),
        me, n, acc, tmp, sbuf, rbuf, ss, sr,
    )
    normed, inverse = layer_norm(middle[...] + acc[...] + bias[...])
    acc[...] = normed
    dres = norm_back(cot[...], normed, inverse, gain[...])
    dres_o[...] = dres
    rows_o[me] = dres.astype(BF)

    def between():
        hidden_o[...] = acc[...] * gain[...] + nbias[...]
        sums_o[0:1, :] = jnp.sum(cot[...] * acc[...], axis=0, keepdims=True)
        sums_o[1:2, :] = jnp.sum(cot[...], axis=0, keepdims=True)
        sums_o[2:3, :] = jnp.sum(dres_o[...], axis=0, keepdims=True)

    chain_gather(rows_o, me, n, gs, gr, between)
    finish()


def mid_back_kernel(
    n, dpre, up, dres_two, normed, inverse, gain,
    dres_o, sums_o, rows_o,
    acc, tmp, sbuf, rbuf, ss, sr, gs, gr,
):
    me = lax.axis_index("tensor")
    rows = normed.shape[0]
    chain_barrier(me, n)
    finish = chain_reduce(
        lambda block: nt_dot(row_block(dpre, block, rows), up[...]),
        me, n, acc, tmp, sbuf, rbuf, ss, sr,
    )
    acc[...] += dres_two[...]
    dres = norm_back(acc[...], normed[...], inverse[...], gain[...])
    dres_o[...] = dres
    rows_o[me] = dres.astype(BF)

    def between():
        sums_o[0:1, :] = jnp.sum(acc[...] * normed[...], axis=0, keepdims=True)
        sums_o[1:2, :] = jnp.sum(acc[...], axis=0, keepdims=True)
        sums_o[2:3, :] = jnp.sum(dres_o[...], axis=0, keepdims=True)

    chain_gather(rows_o, me, n, gs, gr, between)
    finish()


def last_kernel(n, dmix, qkv, dres, up_o, acc, tmp, sbuf, rbuf, ss, sr):
    me = lax.axis_index("tensor")
    rows = dres.shape[0]
    chain_barrier(me, n)

    def term(block):
        return sum(nt_dot(row_block(dmix.at[j], block, rows), qkv[j]) for j in range(3))

    finish = chain_reduce(term, me, n, acc, tmp, sbuf, rbuf, ss, sr)
    up_o[...] = dres[...] + acc[...]
    finish()


def run(body, number, outs, scratch, flops, *operands):
    vmem = pl.BlockSpec(memory_space=pltpu.VMEM)
    return pl.pallas_call(
        body,
        out_shape=[jax.ShapeDtypeStruct(shape, dtype) for shape, dtype in outs],
        in_specs=[vmem] * len(operands),
        out_specs=[vmem] * len(outs),
        scratch_shapes=scratch,
        cost_estimate=pl.CostEstimate(flops=flops, bytes_accessed=60_000_000, transcendentals=0),
        compiler_params=pltpu.CompilerParams(
            collective_id=number, has_side_effects=True, vmem_limit_bytes=40 * 2**20
        ),
    )(*operands)


def reduce_scratch(n, rows, width):
    return [
        pltpu.VMEM((rows, width), F32),
        pltpu.VMEM((rows, width), F32),
        pltpu.VMEM((2, n - 1, rows, width), BF),
        pltpu.VMEM((2, n - 1, rows, width), BF),
    ] + chain_sems(n)


def chain_sems(n):
    return [pltpu.SemaphoreType.DMA((2, n - 1)), pltpu.SemaphoreType.DMA((2, n - 1))]


def per_device(
    inputs,
    lengths,
    qkv_weight,
    qv_bias,
    proj_weight,
    branch_bias,
    up_weight,
    up_bias,
    down_weight,
    norm_gain,
    norm_bias,
    cotangent,
):
    n = lax.axis_size("tensor")
    dp = lax.axis_size("dp")
    own_rows, width = inputs.shape
    seq_count = lengths.shape[0]
    local = qkv_weight.shape[3]
    head_count = local // HD
    head_shape = (seq_count, L, head_count, HD)
    key_valid = jnp.arange(L, dtype=jnp.int32)[None, :] < lengths[:, None]
    total_rows = own_rows * n
    own = (own_rows, width)
    spread = ((n, own_rows, width), BF)
    sums = ((3, width), F32)
    up_full = lax.all_gather(up_weight[0], "dp", axis=0, tiled=True)
    down_full = lax.all_gather(down_weight[0], "dp", axis=1, tiled=True)
    rounded, qkv_blocks, proj_blocks = run(
        functools.partial(front_kernel, n, dp),
        0,
        [spread, ((dp,) + qkv_weight.shape[1:], BF), ((dp,) + proj_weight.shape[1:], BF)],
        chain_sems(n)
        + [pltpu.SemaphoreType.DMA((2, dp)), pltpu.SemaphoreType.DMA((2, dp))],
        0,
        inputs,
        qkv_weight[0],
        proj_weight[0],
    )
    rounded = rounded.reshape(total_rows, width)
    qkv_full = qkv_blocks.transpose(1, 0, 2, 3).reshape(3, width, local)
    proj_full = proj_blocks.transpose(1, 0, 2).reshape(local, width)
    mixed_rows = jnp.einsum("rd,jde->jre", rounded, qkv_full, preferred_element_type=F32)
    queries = (mixed_rows[0] + qv_bias[0, 0]).astype(BF).reshape(head_shape)
    key_rows = mixed_rows[1].astype(BF).reshape(head_shape)
    values = (mixed_rows[2] + qv_bias[0, 1]).astype(BF).reshape(head_shape)
    scores = score_block(queries, key_rows, key_valid)
    row_peak = jnp.max(scores, axis=-1, keepdims=True)
    log_total = row_peak + jnp.log(jnp.sum(jnp.exp(scores - row_peak), axis=-1, keepdims=True))
    soft_weights = jnp.exp(scores - log_total).astype(BF)
    context = (
        jnp.einsum("shqk,skhc->sqhc", soft_weights, values, preferred_element_type=F32)
        .astype(BF)
        .reshape(total_rows, local)
    )
    normed_one, inverse_one, middle, middle_rows = run(
        functools.partial(attn_out_kernel, n),
        1,
        [(own, F32), ((own_rows, 1), F32), (own, F32), spread],
        reduce_scratch(n, own_rows, width) + chain_sems(n),
        2 * total_rows * local * width,
        context,
        proj_full,
        inputs,
        branch_bias[0, 0:1],
        norm_gain[0, 0:1],
        norm_bias[0, 0:1],
    )
    middle_rows = middle_rows.reshape(total_rows, width)
    pre_act = jnp.dot(middle_rows, up_full, preferred_element_type=F32) + up_bias[0]
    active = gelu_value(pre_act).astype(BF)
    hidden, dres_two, sums_two, dres_two_all = run(
        functools.partial(turn_kernel, n),
        2,
        [(own, F32), (own, F32), sums, spread],
        reduce_scratch(n, own_rows, width) + chain_sems(n),
        2 * total_rows * width * active.shape[1],
        active,
        down_full,
        middle,
        branch_bias[0, 1:2],
        norm_gain[0, 1:2],
        norm_bias[0, 1:2],
        cotangent,
    )
    dres_two_all = dres_two_all.reshape(total_rows, width)
    dpre = jnp.einsum(
        "rd,fd->rf", dres_two_all, down_full, preferred_element_type=F32
    ) * gelu_slope(pre_act)
    upbias_part = jnp.sum(dpre, axis=0)
    dpre_b = dpre.astype(BF)
    down_part = jnp.einsum("rf,rd->fd", active, dres_two_all, preferred_element_type=F32)
    up_part = jnp.einsum("rd,rf->df", middle_rows, dpre_b, preferred_element_type=F32)
    up_out = lax.psum_scatter(up_part.astype(BF), "dp", scatter_dimension=0, tiled=True)
    down_out = lax.psum_scatter(down_part.astype(BF), "dp", scatter_dimension=1, tiled=True)
    dres_one, sums_one, dres_one_all = run(
        functools.partial(mid_back_kernel, n),
        3,
        [(own, F32), sums, spread],
        reduce_scratch(n, own_rows, width) + chain_sems(n),
        2 * total_rows * width * dpre_b.shape[1],
        dpre_b,
        up_full,
        dres_two,
        normed_one,
        inverse_one,
        norm_gain[0, 0:1],
    )
    dres_one_all = dres_one_all.reshape(total_rows, width)
    proj_part = jnp.einsum("rc,rd->cd", context, dres_one_all, preferred_element_type=F32)
    dcontext = (
        jnp.einsum("rd,cd->rc", dres_one_all, proj_full, preferred_element_type=F32)
        .astype(BF)
        .reshape(head_shape)
    )
    scores = score_block(queries, key_rows, key_valid)
    probs_full = jnp.exp(scores - log_total)
    dprob = jnp.einsum("sqhc,skhc->shqk", dcontext, values, preferred_element_type=F32)
    dscore = (
        probs_full
        * (dprob - jnp.sum(probs_full * dprob, axis=-1, keepdims=True))
        * (1.0 / math.sqrt(HD))
    ).astype(BF)
    dquery = jnp.einsum("shqk,skhc->sqhc", dscore, key_rows, preferred_element_type=F32)
    dkey = jnp.einsum("shqk,sqhc->skhc", dscore, queries, preferred_element_type=F32)
    dvalue = jnp.einsum("shqk,sqhc->skhc", probs_full.astype(BF), dcontext, preferred_element_type=F32)
    dmixed_full = jnp.stack([dquery, dkey, dvalue]).reshape(3, total_rows, local)
    qvbias_part = jnp.stack([jnp.sum(dmixed_full[0], axis=0), jnp.sum(dmixed_full[2], axis=0)])
    dmixed = dmixed_full.astype(BF)
    qkv_part = jnp.einsum("rd,jre->jde", rounded, dmixed, preferred_element_type=F32)
    upstream = run(
        functools.partial(last_kernel, n),
        4,
        [(own, F32)],
        reduce_scratch(n, own_rows, width),
        6 * total_rows * local * width,
        dmixed,
        qkv_full,
        dres_one,
    )[0]
    qkv_out = lax.psum_scatter(qkv_part.astype(BF), "dp", scatter_dimension=1, tiled=True)
    proj_out = lax.psum_scatter(proj_part.astype(BF), "dp", scatter_dimension=1, tiled=True)
    qvbias_out, upbias_out = lax.psum((qvbias_part, upbias_part), "dp")
    all_sums = lax.psum(jnp.stack([sums_one, sums_two], axis=1), ("dp", "tensor"))
    gain_out, normbias_out, branch_out = all_sums[0], all_sums[1], all_sums[2]
    return (
        hidden,
        upstream,
        qkv_out.astype(F32)[None],
        qvbias_out[None],
        proj_out.astype(F32)[None],
        branch_out[None],
        up_out.astype(F32)[None],
        upbias_out[None],
        down_out.astype(F32)[None],
        gain_out[None],
        normbias_out[None],
    )


def solution(mesh):
    placed = (
        P(("dp", "tensor"), None),
        P("dp"),
        P(None, None, "dp", "tensor"),
        P(None, None, "tensor"),
        P(None, "tensor", "dp"),
        P(),
        P(None, "dp", "tensor"),
        P(None, "tensor"),
        P(None, "tensor", "dp"),
        P(),
        P(),
        P(("dp", "tensor"), None),
    )
    return jax.shard_map(
        per_device,
        mesh=mesh,
        in_specs=placed,
        out_specs=(
            P(("dp", "tensor"), None),
            P(("dp", "tensor"), None),
            P(None, None, "dp", "tensor"),
            P(None, None, "tensor"),
            P(None, "tensor", "dp"),
            P(),
            P(None, "dp", "tensor"),
            P(None, "tensor"),
            P(None, "tensor", "dp"),
            P(),
            P(),
        ),
        check_vma=False,
    )
```

time: 423 us -> 324 us (0.77)
  Pallas kernels: 0 us -> 144 us
  waiting for transfers between devices: 176 us -> 44.9 us
  blocking collectives: 149 us -> 54.8 us
  matrix products: 46.7 us -> 31.5 us
  other arithmetic: 14.9 us -> 4.91 us
  local copies, waits for them, and re-layouts: 18 us -> 27.2 us
    pallas_call x0 -> x5, Pallas kernels: none -> 144 us  [run(): pl.pallas_call(body, out_shape=[jax.ShapeDtypeStruct(shape, dtype) for sh...]
    reduce_scatter x6 -> x2, waiting for transfers between devices: 157 us -> 43.4 us  [the longest x1 38.2 us: per_device(): lax.psum_scatter(up_part.astype(BF), 'dp', scatter_dimension=0, tiled=True)]
    all_gather x6 -> x0, blocking collectives: 98.5 us -> none  [the longest x2 40.1 us: gather_rows(): return lax.all_gather(block_rows, 'tensor', axis=0, tiled=True)]
    unnamed x12 -> x8, waiting for transfers between devices: 15 us -> 1.45 us
    dot_general x15 -> x12, matrix products: 42.4 us -> 29.8 us  [the longest x1 6.71 us: per_device(): jnp.einsum('shqk,skhc->sqhc', dscore, key_rows, preferred_element_type=F32)]
    unnamed x90 -> x92, local copies, waits for them, and re-layouts: 13.2 us -> 22.2 us
    reduce_sum x7 -> x0, other arithmetic: 8.51 us -> none  [the longest x2 2.53 us: layer_norm(): centred = residual - jnp.mean(residual, axis=-1, keepdims=True)]
    all_gather x2, waiting for transfers between devices: 4.32 us -> 0.02 us  [the longest x1 0.02 us: per_device(): up_full = lax.all_gather(up_weight[0], 'dp', axis=0, tiled=True)]
  transfers between devices with their start and end apart: 10 -> 6, of which waited for: 7 -> 2; matrix products, arithmetic and copies ran while one was open for 11% -> 14% of each run, Pallas kernels for 0% -> 25%
where the time goes in v1:
time: 324 us; the launch traced here: 323 us
  Pallas kernels  144 us (44%)
  blocking collectives  54.8 us (17%)
  waiting for transfers between devices  44.9 us (14%)
  matrix products  31.5 us (10%)
  local copies, waits for them, and re-layouts  27.2 us (8%)
  between operations  15.5 us (5%)
  other arithmetic  4.91 us (2%)
    pallas_call x5, Pallas kernels, run(): pl.pallas_call(body, out_shape=[jax.ShapeDtypeStruct(shape, dtype) for sh...  144 us
    psum x1, blocking collectives, per_device(): lax.psum(jnp.stack([sums_one, sums_two], axis=1), ('dp', 'tensor'))  42 us
    reduce_scatter x1, waiting for transfers between devices, per_device(): lax.psum_scatter(up_part.astype(BF), 'dp', scatter_dimension=0, tiled=True)  38.2 us
    unnamed x92, local copies, waits for them, and re-layouts  22.2 us
    psum x1, blocking collectives, per_device(): qvbias_out, upbias_out = lax.psum((qvbias_part, upbias_part), 'dp')  12.8 us
    dot_general x1, matrix products, per_device(): jnp.einsum('shqk,skhc->sqhc', dscore, key_rows, preferred_element_type=F32)  6.71 us
    dot_general x1, matrix products, per_device(): jnp.einsum('shqk,sqhc->skhc', dscore, queries, preferred_element_type=F32)  6.65 us
  transfers between devices with their start and end apart: 6, of which 2 were waited for; matrix products, arithmetic and copies ran while one was open for 14% of the time, Pallas kernels for 25%

profile of v1, /device:TPU:0, one launch (start us, length us, event | category | flops | bytes accessed | tf_op | source)
XLA Modules:
  0.0 323.4 jit_solution(12171820986196826072)
XLA Ops:
  9.4 1.0 copy-done
  10.4 0.9 copy-done.16
  12.1 23.3 %shard_map.203 = (bf16[4,128,768]{2,1,0:T(8,128)(2,1)S(1)}, bf16[8,3,96,192]{3,2,1,0:T(8,128)(2,1)S(1)}, bf16[8,192,96]{2,1,0:T(8,128)(2,1)S(1)}) custom-call(f32[128,768]{1,0:T(8,128)S(1)} %copy-done, bf16[3,96,192]{2,1,0:T(8,128)(2,1)S(1)} %bitcast.112, bf16[192,96]{1,0:T(8,128)(2,1)S(1)} %bitcast.113), custom_call_target="tpu_custom_call" | custom-call | bytes 60000000 | tf_op jit(solution)/shard_map/pallas_call | solution.py:302
  35.5 0.9 convolution_bitcast_fusion
  36.6 1.0 copy.60
  37.6 1.3 reshape.175.proj
  39.8 0.9 fusion.4
  42.9 34.8 %shard_map.204 = (f32[128,768]{1,0:T(8,128)S(1)}, f32[128,1]{1,0:T(8,128)S(1)}, f32[128,768]{1,0:T(8,128)S(1)}, bf16[4,128,768]{2,1,0:T(8,128)(2,1)S(1)}) custom-call(bf16[512,192]{1,0:T(8,128)(2,1)S(1)} %copy.61.ctx, bf16[192,768]{1,0:T(8,128)(2,1)S(1)} %reshape.175.proj, f32[128,768]{1,0:T(8,128)S(1)} %copy-done.1, f32[1,768]{1,0:T(1,128)S(1)} %get-tuple-element.92.bias, ...), custom_call_target="tpu_custom_call" | custom-call | flops 150994944 | bytes 60000000 | tf_op jit(solution)/shard_map/pallas_call | solution.py:302
  80.1 1.6 copy.62
  81.8 2.5 multiply_convert_fusion.1
  84.3 31.7 %shard_map.205 = (f32[128,768]{1,0:T(8,128)S(1)}, f32[128,768]{1,0:T(8,128)S(1)}, f32[3,768]{1,0:T(4,128)S(1)}, bf16[4,128,768]{2,1,0:T(8,128)(2,1)S(1)}) custom-call(bf16[512,768]{1,0:T(8,128)(2,1)S(1)} %get-tuple-element.95.act, bf16[768,768]{1,0:T(8,128)(2,1)S(1)} %bitcast.104, f32[128,768]{1,0:T(8,128)S(1)} %copy-done.9, ...), custom_call_target="tpu_custom_call" | custom-call | flops 603979776 | bytes 60000000 | tf_op jit(solution)/shard_map/pallas_call | solution.py:302
  116.8 1.1 fusion.35
  118.4 32.9 %shard_map.206 = (f32[128,768]{1,0:T(8,128)S(1)}, f32[3,768]{1,0:T(4,128)S(1)}, bf16[4,128,768]{2,1,0:T(8,128)(2,1)S(1)}) custom-call(bf16[512,768]{1,0:T(8,128)(2,1)S(1)} %get-tuple-element.77.dpre, bf16[768,768]{1,0:T(8,128)(2,1)S(1)} %bitcast.107, f32[128,768]{1,0:T(8,128)S(1)} %get-tuple-element.32.dres_two, f32[128,768]{1,0:T(8,128)S(1)} %copy-done.15, ...), custom_call_target="tpu_custom_call" | custom-call | flops 603979776 | bytes 60000000 | tf_op jit(solution)/shard_map/pallas_call | solution.py:302
  152.2 1.0 fusion.38
  153.2 2.4 fusion.28
  155.6 0.9 copy.82
  156.8 6.7 %fusion.23 = bf16[3,64,512]{2,1,0:T(8,128)(2,1)S(1)} fusion(f32[3,512,512]{1,2,0:T(8,128)} %fusion.28, f32[512,3,64]{0,2,1:T(8,128)S(1)} %bitcast.122, f32[3,64]{1,0:T(4,128)S(1)} %add.68, f32[3,512,512]{1,2,0:T(8,128)} %copy-done.20, f32[3,512]{1,0:T(4,128)S(1)} %log_add_fusion, pred[512]{0:T(512)(128)(4,1)S(1)} %copy-done.39), kind=kOutput, calls=%fused_computation.30 | convolution fusion | flops 109611008 | bytes 6888704 | tf_op jit(solution)/shard_map/shqk,sqhc->skhc/dot_general | solution.py:452
  163.6 6.7 %fusion.37 = (f32[3,64]{1,0:T(4,128)S(1)}, bf16[1,512,3,64]{1,3,2,0:T(8,128)(2,1)S(1)}) fusion(bf16[512,3,64]{0,2,1:T(8,128)(2,1)S(1)} %bitcast.129, f32[3,512,512]{1,2,0:T(8,128)} %fusion.28, f32[3,512]{1,0:T(4,128)S(1)} %log_add_fusion, f32[3,512,512]{1,2,0:T(8,128)} %copy-done.20, pred[512]{0:T(512)(128)(4,1)S(1)} %copy-done.39), kind=kOutput, calls=%fused_computation.64 | convolution fusion | flops 109512512 | bytes 6692096 | tf_op jit(solution)/shard_map/shqk,skhc->sqhc/dot_general | solution.py:451
  170.5 1.7 fusion.18
  172.1 3.5 %copy.80 = bf16[3,768,192]{2,0,1:T(4,128)(2,1)} copy(bf16[3,768,192]{1,2,0:T(8,128)(2,1)} %fusion.18) | data formatting | bytes 1769472
  175.7 4.1 %reshape.187 = bf16[768,576]{1,0:T(8,128)(2,1)} reshape(bf16[768,3,192]{2,1,0:T(4,128)(2,1)} %bitcast.120) | data formatting | bytes 1769472
  179.8 3.1 convolution_convert_fusion
  183.0 3.0 convolution_convert_fusion.1
  186.1 42.0 %psum.22 = f32[3,2,768]{2,0,1:T(4,128)S(1)} all-reduce(f32[3,2,768]{2,0,1:T(4,128)S(1)} %pad_maximum_fusion.1), channel_id=1, replica_groups=mesh['dp'=8,'tensor'=4] {'dp','tensor'}, use_global_device_ids=true, to_apply=%region_8.9 | all-reduce | flops 4608 | bytes 36864 | tf_op jit(solution)/shard_map/psum | solution.py:471
  230.2 21.6 %shard_map.207 = f32[128,768]{1,0:T(8,128)S(1)} custom-call(bf16[3,512,192]{2,1,0:T(8,128)(2,1)S(1)} %pad_maximum_fusion.dmix, bf16[3,768,192]{2,1,0:T(8,128)(2,1)S(1)} %bitcast.103, f32[128,768]{1,0:T(8,128)S(1)} %copy-done.13), custom_call_target="tpu_custom_call" | custom-call | flops 452984832 | bytes 60000000 | tf_op jit(solution)/shard_map/pallas_call | solution.py:302
  251.9 12.8 %all-reduce = (f32[1,2,192]{2,1,0:T(2,128)}, f32[1,768]{1,0:T(1,128)}) all-reduce(f32[1,2,192]{2,1,0:T(2,128)S(1)} %maximum_bitcast_fusion, f32[1,768]{1,0:T(1,128)S(1)} %broadcast_in_dim.62), channel_id=1, replica_groups=mesh['dp'=8,'tensor'=4] {'dp'}, use_global_device_ids=true, to_apply=%region_6.7 | all-reduce | flops 1152 | bytes 9216 | tf_op jit(solution)/shard_map/psum | solution.py:470
  264.7 0.9 copy.83
  266.2 1.0 reshape.188
  268.4 5.2 %reduce-scatter.11.cloned.1.call-done = bf16[768,96]{0,1:T(8,128)(2,1)} async-done(((bf16[768,768]{0,1:T(8,128)(2,1)}), bf16[768,96]{0,1:T(8,128)(2,1)}) %reduce-scatter.11.cloned.1.call-update) | async-done | bytes 147472 | tf_op jit(solution)/shard_map/reduce_scatter | solution.py:422
  273.5 1.6 bitcast_convert_fusion
  275.2 38.2 %reduce-scatter.9.cloned.1.call-done = bf16[96,768]{1,0:T(8,128)(2,1)} async-done(((bf16[768,768]{1,0:T(8,128)(2,1)}), bf16[96,768]{1,0:T(8,128)(2,1)}) %reduce-scatter.9.cloned.1.call-update) | async-done | bytes 147472 | tf_op jit(solution)/shard_map/reduce_scatter | solution.py:421
  313.4 1.6 bitcast_convert_fusion.1
  (129 shorter events, 15.9 us)
Async XLA Ops:
  7.2 73.0 %all-gather.7.cloned.1.call-start = ((), (), s32[]{:S(2)}) async-start(), calls=%async_computation.7 | async-start | bytes 1327104 | tf_op jit(solution)/shard_map/all_gather | solution.py:355
  7.9 28.5 %copy-start.37 = (f32[1,2,192]{2,1,0:T(2,128)S(1)}, f32[1,2,192]{2,1,0:T(2,128)}, u32[]{:S(2)}) copy-start(f32[1,2,192]{2,1,0:T(2,128)} %param.15) | copy-start | bytes 4612
  7.9 73.8 %all-gather.5.cloned.1.call-start = ((), (), s32[]{:S(2)}) async-start(), calls=%async_computation.6 | async-start | bytes 1327104 | tf_op jit(solution)/shard_map/all_gather | solution.py:354
  8.7 256.0 %reduce-scatter.15.cloned.1.call-start = ((), (), s32[]{:S(2)}) async-start(), calls=%async_computation.9 | async-start | bytes 442368
  39.0 1.8 copy-start.29
  39.0 2.5 copy-start.38
  39.1 2.5 copy-start.24
  40.7 1.7 copy-start.20
  42.4 35.3 %copy-start.31 = (bf16[3,64,512]{2,1,0:T(8,128)(2,1)}, bf16[3,64,512]{2,1,0:T(8,128)(2,1)S(1)}, u32[]{:S(2)}) copy-start(bf16[3,64,512]{2,1,0:T(8,128)(2,1)S(1)} %convolution_convert_fusion.4) | copy-start | bytes 589828
  81.7 2.6 copy-start.7
  81.8 2.6 copy-start.9
  81.8 35.0 %copy-start.26 = (bf16[1,768,768]{1,2,0:T(8,128)(2,1)S(1)}, bf16[1,768,768]{1,2,0:T(8,128)(2,1)}, u32[]{:S(2)}) copy-start(bf16[1,768,768]{1,2,0:T(8,128)(2,1)} %all-gather.7.cloned.1.call-done) | copy-start | bytes 3538948
  84.3 33.6 %copy-start.3 = (bf16[512,768]{1,0:T(8,128)(2,1)}, bf16[512,768]{1,0:T(8,128)(2,1)S(1)}, u32[]{:S(2)}) copy-start(bf16[512,768]{1,0:T(8,128)(2,1)S(1)} %get-tuple-element.95.act) | copy-start | bytes 2359300
  116.8 1.6 copy-start.2
  116.8 1.6 copy-start.15
  117.9 35.2 %copy-start.5 = (bf16[512,768]{1,0:T(8,128)(2,1)}, bf16[512,768]{1,0:T(8,128)(2,1)S(1)}, u32[]{:S(2)}) copy-start(bf16[512,768]{1,0:T(8,128)(2,1)S(1)} %get-tuple-element.77.dpre) | copy-start | bytes 2359300
  117.9 33.9 %copy-start.32 = (bf16[3,64,512]{2,1,0:T(8,128)(2,1)S(1)}, bf16[3,64,512]{2,1,0:T(8,128)(2,1)}, u32[]{:S(2)}) copy-start(bf16[3,64,512]{2,1,0:T(8,128)(2,1)} %copy-done.31) | copy-start | bytes 589828
  117.9 34.2 %copy-start.21 = (f32[3,512,512]{1,2,0:T(8,128)S(1)}, f32[3,512,512]{1,2,0:T(8,128)}, u32[]{:S(2)}) copy-start(f32[3,512,512]{1,2,0:T(8,128)} %copy-done.20) | copy-start | bytes 9437188
  117.9 34.2 %copy-start.39 = (pred[512]{0:T(512)(128)(4,1)S(1)}, pred[512]{0:T(512)(128)(4,1)}, u32[]{:S(2)}) copy-start(pred[512]{0:T(512)(128)(4,1)} %copy-done.38) | copy-start | bytes 1540
  151.4 1.8 copy-start.12
  151.4 1.8 copy-start.25
  153.2 3.6 %copy-start.23 = (f32[1,512,192]{1,2,0:T(8,128)S(1)}, f32[1,512,192]{1,2,0:T(8,128)}, u32[]{:S(2)}) copy-start(f32[1,512,192]{1,2,0:T(8,128)} %copy-done.22) | copy-start | bytes 1179652
  156.6 109.7 %reduce-scatter.13.cloned.1.call-start = ((), (), s32[]{:S(2)}) async-start(), calls=%async_computation.8 | async-start | bytes 1105920
  156.8 6.8 %copy-start.30 = (bf16[1,512,192]{1,2,0:T(8,128)(2,1)S(1)}, bf16[1,512,192]{1,2,0:T(8,128)(2,1)}, u32[]{:S(2)}) copy-start(bf16[1,512,192]{1,2,0:T(8,128)(2,1)} %copy-done.29) | copy-start | bytes 589828
  170.5 5.2 %copy-start.27 = (bf16[1,512,192]{2,1,0:T(8,128)(2,1)}, bf16[1,512,192]{2,1,0:T(8,128)(2,1)S(1)}, u32[]{:S(2)}) copy-start(bf16[1,512,192]{2,1,0:T(8,128)(2,1)S(1)} %copy.66) | copy-start | bytes 589828
  172.1 7.7 %copy-start.4 = (bf16[512,768]{1,0:T(8,128)(2,1)S(1)}, bf16[512,768]{1,0:T(8,128)(2,1)}, u32[]{:S(2)}) copy-start(bf16[512,768]{1,0:T(8,128)(2,1)} %copy-done.3) | copy-start | bytes 2359300
  179.8 3.2 %copy-start.6 = (bf16[512,768]{1,0:T(8,128)(2,1)S(1)}, bf16[512,768]{1,0:T(8,128)(2,1)}, u32[]{:S(2)}) copy-start(bf16[512,768]{1,0:T(8,128)(2,1)} %copy-done.5) | copy-start | bytes 2359300
  179.8 93.8 %reduce-scatter.11.cloned.1.call-start = ((), (), s32[]{:S(2)}) async-start(), calls=%async_computation.5 | async-start | bytes 1327104 | tf_op jit(solution)/shard_map/reduce_scatter | solution.py:422
  182.9 47.1 %copy-start.28 = (bf16[1,512,192]{2,1,0:T(8,128)(2,1)S(1)}, bf16[1,512,192]{2,1,0:T(8,128)(2,1)}, u32[]{:S(2)}) copy-start(bf16[1,512,192]{2,1,0:T(8,128)(2,1)} %copy-done.27) | copy-start | bytes 589828
  182.9 47.3 %copy-start.13 = (f32[128,768]{1,0:T(8,128)S(1)}, f32[128,768]{1,0:T(8,128)}, u32[]{:S(2)}) copy-start(f32[128,768]{1,0:T(8,128)} %copy-done.12) | copy-start | bytes 1179652
  182.9 130.5 %reduce-scatter.9.cloned.1.call-start = ((), (), s32[]{:S(2)}) async-start(), calls=%async_computation.4 | async-start | bytes 1327104 | tf_op jit(solution)/shard_map/reduce_scatter | solution.py:421
  230.2 84.9 %copy-start.11 = (f32[128,768]{1,0:T(8,128)S(1)}, f32[128,768]{1,0:T(8,128)}, u32[]{:S(2)}) copy-start(f32[128,768]{1,0:T(8,128)} %copy-done.10) | copy-start | bytes 1179652
  (14 other events, 13.7 us)
Sparse Core Ops, SparseCore 0:
  9.9 31.9 all-gather.6
  43.7 24.0 all-gather.4
  156.7 37.4 reduce-scatter.14
  197.2 35.8 reduce-scatter.12
  236.5 36.9 reduce-scatter.10
  276.6 36.7 reduce-scatter.8

commit v2 on v1

--- a/solution.py
+++ b/solution.py
@@ -85,6 +85,46 @@
     @pl.when(jnp.logical_not(inner))
     def _():
         pl.semaphore_wait(barrier, 1 + extra)
+
+
+def group_signal(axis, size):
+    mine = lax.axis_index(axis)
+    for k in range(1, size):
+        pl.semaphore_signal(
+            pltpu.get_barrier_semaphore(),
+            inc=1,
+            device_id={axis: lax.rem(mine + k, size)},
+            device_id_type=MESH,
+        )
+
+
+def owners_copy(part, got, ssem, rsem, slot, dp, k):
+    target = lax.rem(lax.axis_index("dp") + k, dp)
+    return send(part.at[target], got.at[k], ssem.at[slot, k], rsem.at[slot, k], "dp", target)
+
+
+def owners_sum(parts, gots, outs, ssem, rsem, dp):
+    mine = lax.axis_index("dp")
+    for slot, (part, got, out) in enumerate(zip(parts, gots, outs)):
+        out[...] = part[mine].astype(F32)
+        for k in range(1, dp):
+            owners_copy(part, got, ssem, rsem, slot, dp, k).wait()
+            out[...] += got[k].astype(F32)
+
+
+def share_copy(got, ssem, rsem, slot, axis, size, k):
+    mine = lax.axis_index(axis)
+    target = lax.rem(mine + k, size)
+    return send(got.at[mine], got.at[mine], ssem.at[slot, k], rsem.at[slot, k], axis, target)
+
+
+def share_sum(got, ssem, rsem, slot, axis, size):
+    for k in range(1, size):
+        share_copy(got, ssem, rsem, slot, axis, size, k).wait()
+    total = got[0]
+    for k in range(1, size):
+        total = total + got[k]
+    return total
 
 
 def ways(me, n):
@@ -259,13 +299,18 @@
 
 
 def mid_back_kernel(
-    n, dpre, up, dres_two, normed, inverse, gain,
-    dres_o, sums_o, rows_o,
-    acc, tmp, sbuf, rbuf, ss, sr, gs, gr,
+    n, dp, dpre, up, dres_two, normed, inverse, gain, up_part, down_part,
+    dres_o, sums_o, rows_o, up_o, down_o,
+    acc, tmp, sbuf, rbuf, ss, sr, gs, gr, up_got, down_got, ws, wr,
 ):
     me = lax.axis_index("tensor")
     rows = normed.shape[0]
-    chain_barrier(me, n)
+    group_signal("dp", dp)
+    chain_barrier(me, n, dp - 1)
+    parts, gots, outs = (up_part, down_part), (up_got, down_got), (up_o, down_o)
+    for k in range(1, dp):
+        for slot in range(2):
+            owners_copy(parts[slot], gots[slot], ws, wr, slot, dp, k).start()
     finish = chain_reduce(
         lambda block: nt_dot(row_block(dpre, block, rows), up[...]),
         me, n, acc, tmp, sbuf, rbuf, ss, sr,
@@ -282,19 +327,42 @@
 
     chain_gather(rows_o, me, n, gs, gr, between)
     finish()
-
-
-def last_kernel(n, dmix, qkv, dres, up_o, acc, tmp, sbuf, rbuf, ss, sr):
+    owners_sum(parts, gots, outs, ws, wr, dp)
+
+
+def last_kernel(
+    n, dp, dmix, qkv, dres, qkv_part, proj_part, sums, biases,
+    up_o, qkv_o, proj_o, sums_o, biases_o,
+    acc, tmp, sbuf, rbuf, ss, sr, qkv_got, proj_got, ws, wr, sums_got, biases_got, sums_all, ts, tr,
+):
     me = lax.axis_index("tensor")
+    mine = lax.axis_index("dp")
     rows = dres.shape[0]
-    chain_barrier(me, n)
+    group_signal("dp", dp)
+    group_signal("tensor", n)
+    pl.semaphore_wait(pltpu.get_barrier_semaphore(), dp + n - 2)
+    sums_got[mine] = sums[...]
+    biases_got[mine] = biases[...]
+    parts, gots, outs = (qkv_part, proj_part), (qkv_got, proj_got), (qkv_o, proj_o)
+    for k in range(1, dp):
+        share_copy(sums_got, ws, wr, 2, "dp", dp, k).start()
+        share_copy(biases_got, ws, wr, 3, "dp", dp, k).start()
+    for k in range(1, dp):
+        for slot in range(2):
+            owners_copy(parts[slot], gots[slot], ws, wr, slot, dp, k).start()
 
     def term(block):
         return sum(nt_dot(row_block(dmix.at[j], block, rows), qkv[j]) for j in range(3))
 
     finish = chain_reduce(term, me, n, acc, tmp, sbuf, rbuf, ss, sr)
+    sums_all[me] = share_sum(sums_got, ws, wr, 2, "dp", dp)
+    for k in range(1, n):
+        share_copy(sums_all, ts, tr, 0, "tensor", n, k).start()
+    biases_o[...] = share_sum(biases_got, ws, wr, 3, "dp", dp)
     up_o[...] = dres[...] + acc[...]
+    owners_sum(parts, gots, outs, ws, wr, dp)
     finish()
+    sums_o[...] = share_sum(sums_all, ts, tr, 0, "tensor", n)
 
 
 def run(body, number, outs, scratch, flops, *operands):
@@ -416,15 +484,18 @@
     ) * gelu_slope(pre_act)
     upbias_part = jnp.sum(dpre, axis=0)
     dpre_b = dpre.astype(BF)
-    down_part = jnp.einsum("rf,rd->fd", active, dres_two_all, preferred_element_type=F32)
+    down_part = jnp.einsum("rd,rf->df", dres_two_all, active, preferred_element_type=F32)
     up_part = jnp.einsum("rd,rf->df", middle_rows, dpre_b, preferred_element_type=F32)
-    up_out = lax.psum_scatter(up_part.astype(BF), "dp", scatter_dimension=0, tiled=True)
-    down_out = lax.psum_scatter(down_part.astype(BF), "dp", scatter_dimension=1, tiled=True)
-    dres_one, sums_one, dres_one_all = run(
-        functools.partial(mid_back_kernel, n),
+    units = active.shape[1]
+    shard = width // dp
+    dres_one, sums_one, dres_one_all, up_out, down_turned = run(
+        functools.partial(mid_back_kernel, n, dp),
         3,
-        [(own, F32), sums, spread],
-        reduce_scratch(n, own_rows, width) + chain_sems(n),
+        [(own, F32), sums, spread, ((shard, units), F32), ((shard, units), F32)],
+        reduce_scratch(n, own_rows, width)
+        + chain_sems(n)
+        + [pltpu.VMEM((dp, shard, units), BF)] * 2
+        + [pltpu.SemaphoreType.DMA((2, dp))] * 2,
         2 * total_rows * width * dpre_b.shape[1],
         dpre_b,
         up_full,
@@ -432,9 +503,11 @@
         normed_one,
         inverse_one,
         norm_gain[0, 0:1],
+        up_part.astype(BF).reshape(dp, shard, units),
+        down_part.astype(BF).reshape(dp, shard, units),
     )
     dres_one_all = dres_one_all.reshape(total_rows, width)
-    proj_part = jnp.einsum("rc,rd->cd", context, dres_one_all, preferred_element_type=F32)
+    proj_part = jnp.einsum("rd,rc->dc", dres_one_all, context, preferred_element_type=F32)
     dcontext = (
         jnp.einsum("rd,cd->rc", dres_one_all, proj_full, preferred_element_type=F32)
         .astype(BF)
@@ -454,32 +527,58 @@
     dmixed_full = jnp.stack([dquery, dkey, dvalue]).reshape(3, total_rows, local)
     qvbias_part = jnp.stack([jnp.sum(dmixed_full[0], axis=0), jnp.sum(dmixed_full[2], axis=0)])
     dmixed = dmixed_full.astype(BF)
-    qkv_part = jnp.einsum("rd,jre->jde", rounded, dmixed, preferred_element_type=F32)
-    upstream = run(
-        functools.partial(last_kernel, n),
+    qkv_part = jnp.dot(
+        rounded.T,
+        dmixed.transpose(1, 0, 2).reshape(total_rows, 3 * local),
+        preferred_element_type=F32,
+    )
+    all_sums = jnp.concatenate([sums_one, sums_two], axis=0)
+    biases = jnp.concatenate([qvbias_part.reshape(1, -1), upbias_part.reshape(1, -1)], axis=1)
+    upstream, qkv_turned, proj_turned, all_sums, biases = run(
+        functools.partial(last_kernel, n, dp),
         4,
-        [(own, F32)],
-        reduce_scratch(n, own_rows, width),
+        [
+            (own, F32),
+            ((shard, 3 * local), F32),
+            ((shard, local), F32),
+            (all_sums.shape, F32),
+            (biases.shape, F32),
+        ],
+        reduce_scratch(n, own_rows, width)
+        + [pltpu.VMEM((dp, shard, 3 * local), BF), pltpu.VMEM((dp, shard, local), BF)]
+        + [pltpu.SemaphoreType.DMA((4, dp))] * 2
+        + [
+            pltpu.VMEM((dp,) + all_sums.shape, F32),
+            pltpu.VMEM((dp,) + biases.shape, F32),
+            pltpu.VMEM((n,) + all_sums.shape, F32),
+        ]
+        + [pltpu.SemaphoreType.DMA((1, n))] * 2,
         6 * total_rows * local * width,
         dmixed,
         qkv_full,
         dres_one,
-    )[0]
-    qkv_out = lax.psum_scatter(qkv_part.astype(BF), "dp", scatter_dimension=1, tiled=True)
-    proj_out = lax.psum_scatter(proj_part.astype(BF), "dp", scatter_dimension=1, tiled=True)
-    qvbias_out, upbias_out = lax.psum((qvbias_part, upbias_part), "dp")
-    all_sums = lax.psum(jnp.stack([sums_one, sums_two], axis=1), ("dp", "tensor"))
-    gain_out, normbias_out, branch_out = all_sums[0], all_sums[1], all_sums[2]
+        qkv_part.astype(BF).reshape(dp, shard, 3 * local),
+        proj_part.astype(BF).reshape(dp, shard, local),
+        all_sums,
+        biases,
+    )
+    qkv_out = qkv_turned.reshape(shard, 3, local).transpose(1, 0, 2)
+    proj_out = proj_turned.T
+    down_out = down_turned.T
+    qvbias_out = biases[0, : 2 * local].reshape(2, local)
+    upbias_out = biases[0, 2 * local :]
+    pairs = all_sums.reshape(2, 3, width)
+    gain_out, normbias_out, branch_out = pairs[:, 0], pairs[:, 1], pairs[:, 2]
     return (
         hidden,
         upstream,
-        qkv_out.astype(F32)[None],
+        qkv_out[None],
         qvbias_out[None],
-        proj_out.astype(F32)[None],
+        proj_out[None],
         branch_out[None],
-        up_out.astype(F32)[None],
+        up_out[None],
         upbias_out[None],
-        down_out.astype(F32)[None],
+        down_out[None],
         gain_out[None],
         normbias_out[None],
     )

time: 324 us -> 239 us (0.74)
  blocking collectives: 54.8 us -> 0 us
  waiting for transfers between devices: 44.9 us -> 1.4 us
  Pallas kernels: 144 us -> 156 us
  local copies, waits for them, and re-layouts: 27.2 us -> 32.8 us
    psum x2 -> x0, blocking collectives: 54.8 us -> none  [the longest x1 42 us: per_device(): lax.psum(jnp.stack([sums_one, sums_two], axis=1), ('dp', 'tensor'))]
    reduce_scatter x2 -> x0, waiting for transfers between devices: 43.4 us -> none  [the longest x1 38.2 us: per_device(): lax.psum_scatter(up_part.astype(BF), 'dp', scatter_dimension=0, tiled=True)]
    pallas_call x5, Pallas kernels: 144 us -> 156 us  [run(): pl.pallas_call(body, out_shape=[jax.ShapeDtypeStruct(shape, dtype) for sh...]
    unnamed x92 -> x89, local copies, waits for them, and re-layouts: 22.2 us -> 17.7 us
    broadcast_in_dim x5 -> x0, other arithmetic: 3.98 us -> none  [the longest x1 1.64 us: per_device(): down_out.astype(F32)[None]]
    another operation x3, local copies, waits for them, and re-layouts: 0.4 us -> 3.66 us  [per_device(): jnp.stack([dquery, dkey, dvalue]).reshape(3, total_rows, local)]
  transfers between devices with their start and end apart: 6 -> 2, of which waited for: 2 -> 0; matrix products, arithmetic and copies ran while one was open for 14% -> 4% of each run, Pallas kernels for 25% -> 24%
where the time goes in v2:
time: 239 us
  Pallas kernels  156 us (65%)
  local copies, waits for them, and re-layouts  32.8 us (14%)
  matrix products  30.1 us (13%)
  between operations  15.3 us (6%)
  other arithmetic  2.86 us (1%)
    pallas_call x5, Pallas kernels, run(): pl.pallas_call(body, out_shape=[jax.ShapeDtypeStruct(shape, dtype) for sh...  156 us
    unnamed x89, local copies, waits for them, and re-layouts  17.7 us
    dot_general x1, matrix products, per_device(): jnp.einsum('shqk,skhc->sqhc', dscore, key_rows, preferred_element_type=F32)  7.21 us
    dot_general x1, matrix products, per_device(): jnp.einsum('shqk,sqhc->skhc', dscore, queries, preferred_element_type=F32)  6.65 us
  transfers between devices with their start and end apart: 2, of which 0 were waited for; matrix products, arithmetic and copies ran while one was open for 4% of the time, Pallas kernels for 24%

profile of v2, /device:TPU:0, one launch (start us, length us, event | category | flops | bytes accessed | tf_op | source)
XLA Modules:
  0.0 238.7 jit_solution(15819696053999849207)
XLA Ops:
  9.3 1.0 copy-done
  10.3 0.9 copy-done.17
  12.0 23.3 %shard_map.203 = (bf16[4,128,768]{2,1,0:T(8,128)(2,1)S(1)}, bf16[8,3,96,192]{3,2,1,0:T(8,128)(2,1)S(1)}, bf16[8,192,96]{2,1,0:T(8,128)(2,1)S(1)}) custom-call(f32[128,768]{1,0:T(8,128)S(1)} %copy-done, bf16[3,96,192]{2,1,0:T(8,128)(2,1)S(1)} %bitcast.121, bf16[192,96]{1,0:T(8,128)(2,1)S(1)} %bitcast.123), custom_call_target="tpu_custom_call" | custom-call | bytes 60000000 | tf_op jit(solution)/shard_map/pallas_call | solution.py:370
  35.5 1.9 convolution_bitcast_fusion
  38.2 1.0 slice.89
  39.2 1.2 fusion.36
  40.5 0.9 fusion.4
  42.2 0.9 convolution_convert_fusion.4
  43.8 34.7 %shard_map.204 = (f32[128,768]{1,0:T(8,128)S(1)}, f32[128,1]{1,0:T(8,128)S(1)}, f32[128,768]{1,0:T(8,128)S(1)}, bf16[4,128,768]{2,1,0:T(8,128)(2,1)S(1)}) custom-call(bf16[512,192]{1,0:T(8,128)(2,1)S(1)} %copy.67.ctx, bf16[192,768]{1,0:T(8,128)(2,1)S(1)} %reshape.202.proj, f32[128,768]{1,0:T(8,128)S(1)} %copy-done.1, f32[1,768]{1,0:T(1,128)S(1)} %get-tuple-element.106.bias, ...), custom_call_target="tpu_custom_call" | custom-call | flops 150994944 | bytes 60000000 | tf_op jit(solution)/shard_map/pallas_call | solution.py:370
  80.1 0.9 copy-done.19
  81.0 1.6 copy.68
  82.6 2.4 %multiply_convert_fusion.1 = (bf16[512,768]{1,0:T(8,128)(2,1)S(1)}, f32[512,768]{1,0:T(8,128)S(1)}) fusion(f32[768]{0:T(1024)S(1)} %reduce.12, bf16[512,768]{1,0:T(8,128)(2,1)} %bitcast.124, bf16[1,768,768]{2,1,0:T(8,128)(2,1)} %all-gather.5.cloned.1.call-done), kind=kOutput, calls=%fused_computation.16 | convolution fusion | flops 606339072 | bytes 4328448 | tf_op jit(solution)/shard_map/dot_general | solution.py:465
  85.1 31.7 %shard_map.205 = (f32[128,768]{1,0:T(8,128)S(1)}, f32[128,768]{1,0:T(8,128)S(1)}, f32[3,768]{1,0:T(4,128)S(1)}, bf16[4,128,768]{2,1,0:T(8,128)(2,1)S(1)}) custom-call(bf16[512,768]{1,0:T(8,128)(2,1)S(1)} %get-tuple-element.109.act, bf16[768,768]{1,0:T(8,128)(2,1)S(1)} %bitcast.107, f32[128,768]{1,0:T(8,128)S(1)} %copy-done.7, ...), custom_call_target="tpu_custom_call" | custom-call | flops 603979776 | bytes 60000000 | tf_op jit(solution)/shard_map/pallas_call | solution.py:370
  118.4 1.1 fusion.35
  120.8 42.2 %shard_map.206 = (f32[128,768]{1,0:T(8,128)S(1)}, f32[3,768]{1,0:T(4,128)S(1)}, bf16[4,128,768]{2,1,0:T(8,128)(2,1)S(1)}, f32[96,768]{1,0:T(8,128)S(1)}, f32[96,768]{1,0:T(8,128)S(1)}) custom-call(bf16[512,768]{1,0:T(8,128)(2,1)S(1)} %get-tuple-element.89.dpre, bf16[768,768]{1,0:T(8,128)(2,1)S(1)} %bitcast.113, f32[128,768]{1,0:T(8,128)S(1)} %get-tuple-element.39.dres_two, ...), custom_call_target="tpu_custom_call" | custom-call | flops 603979776 | bytes 60000000 | tf_op jit(solution)/shard_map/pallas_call | solution.py:370
  163.9 1.6 fusion.38
  165.5 2.4 %fusion.27 = f32[3,512,512]{1,2,0:T(8,128)} fusion(bf16[512,3,64]{0,2,1:T(8,128)(2,1)S(1)} %bitcast.134, f32[512,3,64]{0,2,1:T(8,128)S(1)} %bitcast.131, f32[3,64]{1,0:T(4,128)S(1)} %add.51), kind=kOutput, calls=%fused_computation.38 | convolution fusion | flops 100859904 | bytes 3736320 | tf_op jit(solution)/shard_map/sqhc,skhc->shqk/dot_general | solution.py:518
  167.9 6.7 %fusion.22 = bf16[3,64,512]{2,1,0:T(8,128)(2,1)S(1)} fusion(f32[3,512,512]{1,2,0:T(8,128)} %fusion.27, f32[512,3,64]{0,2,1:T(8,128)S(1)} %bitcast.129, f32[3,64]{1,0:T(4,128)S(1)} %add.54, f32[3,512,512]{1,2,0:T(8,128)} %copy-done.21, f32[3,512]{1,0:T(4,128)S(1)} %log_add_fusion, pred[512]{0:T(512)(128)(4,1)S(1)} %copy-done.39), kind=kOutput, calls=%fused_computation.29 | convolution fusion | flops 109611008 | bytes 6888704 | tf_op jit(solution)/shard_map/shqk,sqhc->skhc/dot_general | solution.py:525
  174.6 7.2 %fusion.37 = (f32[3,64]{1,0:T(4,128)S(1)}, bf16[1,512,3,64]{1,3,2,0:T(8,128)(2,1)}) fusion(bf16[512,3,64]{0,2,1:T(8,128)(2,1)S(1)} %bitcast.136, f32[3,512,512]{1,2,0:T(8,128)} %fusion.27, f32[3,512]{1,0:T(4,128)S(1)} %log_add_fusion, f32[3,512,512]{1,2,0:T(8,128)} %copy-done.21, pred[512]{0:T(512)(128)(4,1)S(1)} %copy-done.39), kind=kOutput, calls=%fused_computation.65 | convolution fusion | flops 109512512 | bytes 6692096 | tf_op jit(solution)/shard_map/shqk,skhc->sqhc/dot_general | solution.py:524
  182.0 1.1 copy.74
  183.3 0.8 copy.73
  184.1 1.8 copy.72
  185.9 2.1 fusion.34
  188.0 2.2 copy.75
  190.2 2.6 %convolution_convert_fusion.2 = bf16[768,576]{0,1:T(8,128)(2,1)} fusion(bf16[512,576]{0,1:T(8,128)(2,1)} %bitcast.139, bf16[512,768]{1,0:T(8,128)(2,1)S(1)} %bitcast.117), kind=kOutput, calls=%fused_computation.23 | convolution fusion | flops 453427200 | bytes 2260992 | tf_op jit(solution)/shard_map/dot_general | solution.py:530
  192.8 1.5 copy.76
  194.4 1.0 copy-done.5
  195.4 24.2 %shard_map.207 = (f32[128,768]{1,0:T(8,128)S(1)}, f32[96,576]{1,0:T(8,128)S(1)}, f32[96,192]{1,0:T(8,128)S(1)}, f32[6,768]{1,0:T(8,128)S(1)}, f32[1,1152]{1,0:T(1,128)S(1)}) custom-call(bf16[3,512,192]{2,1,0:T(8,128)(2,1)S(1)} %get-tuple-element.93.dmix, bf16[3,768,192]{2,1,0:T(8,128)(2,1)S(1)} %bitcast.106, f32[128,768]{1,0:T(8,128)S(1)} %copy-done.5, ...), custom_call_target="tpu_custom_call" | custom-call | flops 452984832 | bytes 60000000 | tf_op jit(solution)/shard_map/pallas_call | solution.py:370
  224.9 1.1 copy.78
  226.0 0.9 copy.79
  226.9 1.8 copy.94
  228.6 1.8 copy.95
  (118 shorter events, 16.8 us)
Async XLA Ops:
  7.2 73.8 %all-gather.7.cloned.1.call-start = ((), (), s32[]{:S(2)}) async-start(), calls=%async_computation.1 | async-start | bytes 1327104 | tf_op jit(solution)/shard_map/all_gather | solution.py:423
  7.9 29.5 %copy-start.36 = (f32[1,2,192]{2,1,0:T(2,128)S(1)}, f32[1,2,192]{2,1,0:T(2,128)}, u32[]{:S(2)}) copy-start(f32[1,2,192]{2,1,0:T(2,128)} %param.15) | copy-start | bytes 4612
  7.9 74.6 %all-gather.5.cloned.1.call-start = ((), (), s32[]{:S(2)}) async-start(), calls=%async_computation | async-start | bytes 1327104 | tf_op jit(solution)/shard_map/all_gather | solution.py:422
  9.3 1.0 copy-start
  39.2 2.9 %copy-start.28 = (bf16[1,512,192]{1,2,0:T(8,128)(2,1)}, bf16[1,512,192]{1,2,0:T(8,128)(2,1)S(1)}, u32[]{:S(2)}) copy-start(bf16[1,512,192]{1,2,0:T(8,128)(2,1)S(1)} %slice.89) | copy-start | bytes 589828
  39.2 3.0 %copy-start.37 = (pred[512]{0:T(512)(128)(4,1)}, pred[512]{0:T(512)(128)(4,1)S(1)}, u32[]{:S(2)}) copy-start(pred[512]{0:T(512)(128)(4,1)S(1)} %iota_compare_fusion) | copy-start | bytes 1540
  40.5 1.7 copy-start.25
  41.4 1.7 copy-start.21
  42.1 1.1 copy-start.35
  42.1 1.2 copy-start.32
  42.2 1.2 copy-start.33
  42.2 1.2 copy-start.34
  42.2 1.6 copy-start.1
  82.6 2.5 %copy-start.3 = (f32[128,768]{1,0:T(8,128)S(1)}, f32[128,768]{1,0:T(8,128)}, u32[]{:S(2)}) copy-start(f32[128,768]{1,0:T(8,128)} %cot.1) | copy-start | bytes 1179652
  82.6 2.5 %copy-start.7 = (f32[128,768]{1,0:T(8,128)S(1)}, f32[128,768]{1,0:T(8,128)}, u32[]{:S(2)}) copy-start(f32[128,768]{1,0:T(8,128)} %copy-done.6) | copy-start | bytes 1179652
  85.0 33.3 %copy-start.27 = (bf16[1,768,768]{1,2,0:T(8,128)(2,1)S(1)}, bf16[1,768,768]{1,2,0:T(8,128)(2,1)}, u32[]{:S(2)}) copy-start(bf16[1,768,768]{1,2,0:T(8,128)(2,1)} %all-gather.7.cloned.1.call-done) | copy-start | bytes 3538948
  118.4 1.1 copy-start.20
  119.5 1.3 copy-start.2
  119.5 1.4 copy-start.11
  120.8 42.7 %copy-start.31 = (bf16[3,64,512]{2,1,0:T(8,128)(2,1)S(1)}, bf16[3,64,512]{2,1,0:T(8,128)(2,1)}, u32[]{:S(2)}) copy-start(bf16[3,64,512]{2,1,0:T(8,128)(2,1)} %copy-done.30) | copy-start | bytes 589828
  120.8 43.0 %copy-start.22 = (f32[3,512,512]{1,2,0:T(8,128)S(1)}, f32[3,512,512]{1,2,0:T(8,128)}, u32[]{:S(2)}) copy-start(f32[3,512,512]{1,2,0:T(8,128)} %copy-done.21) | copy-start | bytes 9437188
  120.8 43.0 %copy-start.38 = (pred[512]{0:T(512)(128)(4,1)S(1)}, pred[512]{0:T(512)(128)(4,1)}, u32[]{:S(2)}) copy-start(pred[512]{0:T(512)(128)(4,1)} %copy-done.37) | copy-start | bytes 1540
  163.0 2.4 %copy-start.4 = (f32[128,768]{1,0:T(8,128)}, f32[128,768]{1,0:T(8,128)S(1)}, u32[]{:S(2)}) copy-start(f32[128,768]{1,0:T(8,128)S(1)} %get-tuple-element.43.dres) | copy-start | bytes 1179652
  163.0 2.4 %copy-start.12 = (f32[96,768]{1,0:T(8,128)}, f32[96,768]{1,0:T(8,128)S(1)}, u32[]{:S(2)}) copy-start(f32[96,768]{1,0:T(8,128)S(1)} %get-tuple-element.52) | copy-start | bytes 884740
  163.0 2.4 %copy-start.14 = (f32[96,768]{1,0:T(8,128)}, f32[96,768]{1,0:T(8,128)S(1)}, u32[]{:S(2)}) copy-start(f32[96,768]{1,0:T(8,128)S(1)} %get-tuple-element.51) | copy-start | bytes 884740
  163.1 2.4 %copy-start.26 = (f32[1,512,192]{1,2,0:T(8,128)S(1)}, f32[1,512,192]{1,2,0:T(8,128)}, u32[]{:S(2)}) copy-start(f32[1,512,192]{1,2,0:T(8,128)} %copy-done.25) | copy-start | bytes 1179652
  163.8 4.1 %copy-start.24 = (f32[1,512,192]{1,2,0:T(8,128)S(1)}, f32[1,512,192]{1,2,0:T(8,128)}, u32[]{:S(2)}) copy-start(f32[1,512,192]{1,2,0:T(8,128)} %copy-done.23) | copy-start | bytes 1179652
  163.8 4.1 %copy-start.39 = (pred[512]{0:T(512)(128)(4,1)S(1)}, pred[512]{0:T(512)(128)(4,1)}, u32[]{:S(2)}) copy-start(pred[512]{0:T(512)(128)(4,1)} %copy-done.37) | copy-start | bytes 1540
  167.9 6.7 %copy-start.29 = (bf16[1,512,192]{1,2,0:T(8,128)(2,1)S(1)}, bf16[1,512,192]{1,2,0:T(8,128)(2,1)}, u32[]{:S(2)}) copy-start(bf16[1,512,192]{1,2,0:T(8,128)(2,1)} %copy-done.28) | copy-start | bytes 589828
  194.4 1.0 copy-start.5
  221.1 9.3 %copy-start.15 = (f32[96,768]{1,0:T(8,128)S(1)}, f32[96,768]{1,0:T(8,128)}, u32[]{:S(2)}) copy-start(f32[96,768]{1,0:T(8,128)} %copy-done.14) | copy-start | bytes 884740
  221.1 10.0 %copy-start.13 = (f32[96,768]{1,0:T(8,128)S(1)}, f32[96,768]{1,0:T(8,128)}, u32[]{:S(2)}) copy-start(f32[96,768]{1,0:T(8,128)} %copy-done.12) | copy-start | bytes 884740
  (10 other events, 7.9 us)
Sparse Core Ops, SparseCore 0:
  9.9 31.8 all-gather.6
  43.7 24.0 all-gather.4

commit v3 on v2

--- a/solution.py
+++ b/solution.py
@@ -328,6 +328,43 @@
     chain_gather(rows_o, me, n, gs, gr, between)
     finish()
     owners_sum(parts, gots, outs, ws, wr, dp)
+
+
+def tn_dot(left, right):
+    return lax.dot_general(left, right, (((0,), (0,)), ((), ())), preferred_element_type=F32)
+
+
+def attn_back_kernel(
+    lengths, dres, proj, ctx, rounded, query, keyrow, value,
+    dmix_o, qkv_o, proj_o, bias_o, dctx,
+):
+    local = ctx.shape[1]
+    scale = 1.0 / math.sqrt(HD)
+    dctx[...] = nt_dot(dres[...], proj[...]).astype(BF)
+    proj_o[...] = tn_dot(dres[...], ctx[...]).astype(BF)
+    for seq in range(ctx.shape[0] // L):
+        rows = slice(seq * L, (seq + 1) * L)
+        valid = lax.broadcasted_iota(jnp.int32, (L, L), 1) < lengths[seq]
+        for head in range(local // HD):
+            cols = slice(head * HD, (head + 1) * HD)
+            q, k, v, dc = query[rows, cols], keyrow[rows, cols], value[rows, cols], dctx[rows, cols]
+            scores = jnp.where(valid, nt_dot(q, k) * scale, -1e30)
+            weights = jnp.exp(scores - jnp.max(scores, axis=-1, keepdims=True))
+            prob = weights * (1.0 / jnp.sum(weights, axis=-1, keepdims=True))
+            dprob = nt_dot(dc, v)
+            inner = jnp.sum(prob * dprob, axis=-1, keepdims=True)
+            dscore = (prob * (dprob - inner) * scale).astype(BF)
+            grads = (
+                jnp.dot(dscore, k, preferred_element_type=F32),
+                tn_dot(dscore, q),
+                tn_dot(prob.astype(BF), dc),
+            )
+            for j, grad in enumerate(grads):
+                spot = slice(j * local + head * HD, j * local + (head + 1) * HD)
+                dmix_o[rows, spot] = grad.astype(BF)
+                total = jnp.sum(grad, axis=0, keepdims=True)
+                bias_o[:, spot] = total if seq == 0 else bias_o[:, spot] + total
+    qkv_o[...] = tn_dot(rounded[...], dmix_o[...]).astype(BF)
 
 
 def last_kernel(
@@ -352,7 +389,7 @@
             owners_copy(parts[slot], gots[slot], ws, wr, slot, dp, k).start()
 
     def term(block):
-        return sum(nt_dot(row_block(dmix.at[j], block, rows), qkv[j]) for j in range(3))
+        return nt_dot(row_block(dmix, block, rows), qkv[...])
 
     finish = chain_reduce(term, me, n, acc, tmp, sbuf, rbuf, ss, sr)
     sums_all[me] = share_sum(sums_got, ws, wr, 2, "dp", dp)
@@ -433,12 +470,15 @@
         proj_weight[0],
     )
     rounded = rounded.reshape(total_rows, width)
-    qkv_full = qkv_blocks.transpose(1, 0, 2, 3).reshape(3, width, local)
+    qkv_full = qkv_blocks.transpose(0, 2, 1, 3).reshape(width, 3 * local)
     proj_full = proj_blocks.transpose(1, 0, 2).reshape(local, width)
-    mixed_rows = jnp.einsum("rd,jde->jre", rounded, qkv_full, preferred_element_type=F32)
-    queries = (mixed_rows[0] + qv_bias[0, 0]).astype(BF).reshape(head_shape)
-    key_rows = mixed_rows[1].astype(BF).reshape(head_shape)
-    values = (mixed_rows[2] + qv_bias[0, 1]).astype(BF).reshape(head_shape)
+    mixed_rows = jnp.dot(rounded, qkv_full, preferred_element_type=F32)
+    queries_2d = (mixed_rows[:, :local] + qv_bias[0, 0]).astype(BF)
+    key_2d = mixed_rows[:, local : 2 * local].astype(BF)
+    values_2d = (mixed_rows[:, 2 * local :] + qv_bias[0, 1]).astype(BF)
+    queries = queries_2d.reshape(head_shape)
+    key_rows = key_2d.reshape(head_shape)
+    values = values_2d.reshape(head_shape)
     scores = score_block(queries, key_rows, key_valid)
     row_peak = jnp.max(scores, axis=-1, keepdims=True)
     log_total = row_peak + jnp.log(jnp.sum(jnp.exp(scores - row_peak), axis=-1, keepdims=True))
@@ -507,33 +547,24 @@
         down_part.astype(BF).reshape(dp, shard, units),
     )
     dres_one_all = dres_one_all.reshape(total_rows, width)
-    proj_part = jnp.einsum("rd,rc->dc", dres_one_all, context, preferred_element_type=F32)
-    dcontext = (
-        jnp.einsum("rd,cd->rc", dres_one_all, proj_full, preferred_element_type=F32)
-        .astype(BF)
-        .reshape(head_shape)
-    )
-    scores = score_block(queries, key_rows, key_valid)
-    probs_full = jnp.exp(scores - log_total)
-    dprob = jnp.einsum("sqhc,skhc->shqk", dcontext, values, preferred_element_type=F32)
-    dscore = (
-        probs_full
-        * (dprob - jnp.sum(probs_full * dprob, axis=-1, keepdims=True))
-        * (1.0 / math.sqrt(HD))
-    ).astype(BF)
-    dquery = jnp.einsum("shqk,skhc->sqhc", dscore, key_rows, preferred_element_type=F32)
-    dkey = jnp.einsum("shqk,sqhc->skhc", dscore, queries, preferred_element_type=F32)
-    dvalue = jnp.einsum("shqk,sqhc->skhc", probs_full.astype(BF), dcontext, preferred_element_type=F32)
-    dmixed_full = jnp.stack([dquery, dkey, dvalue]).reshape(3, total_rows, local)
-    qvbias_part = jnp.stack([jnp.sum(dmixed_full[0], axis=0), jnp.sum(dmixed_full[2], axis=0)])
-    dmixed = dmixed_full.astype(BF)
-    qkv_part = jnp.dot(
-        rounded.T,
-        dmixed.transpose(1, 0, 2).reshape(total_rows, 3 * local),
-        preferred_element_type=F32,
+    vmem = pl.BlockSpec(memory_space=pltpu.VMEM)
+    dmixed, qkv_part, proj_part, mix_sums = pl.pallas_call(
+        attn_back_kernel,
+        out_shape=[
+            jax.ShapeDtypeStruct((total_rows, 3 * local), BF),
+            jax.ShapeDtypeStruct((width, 3 * local), BF),
+            jax.ShapeDtypeStruct((width, local), BF),
+            jax.ShapeDtypeStruct((1, 3 * local), F32),
+        ],
+        in_specs=[pl.BlockSpec(memory_space=pltpu.SMEM)] + [vmem] * 7,
+        out_specs=[vmem] * 4,
+        scratch_shapes=[pltpu.VMEM((total_rows, local), BF)],
+        compiler_params=pltpu.CompilerParams(vmem_limit_bytes=40 * 2**20),
+    )(
+        lengths, dres_one_all, proj_full, context, rounded, queries_2d, key_2d, values_2d
     )
     all_sums = jnp.concatenate([sums_one, sums_two], axis=0)
-    biases = jnp.concatenate([qvbias_part.reshape(1, -1), upbias_part.reshape(1, -1)], axis=1)
+    biases = jnp.concatenate([mix_sums, upbias_part.reshape(1, -1)], axis=1)
     upstream, qkv_turned, proj_turned, all_sums, biases = run(
         functools.partial(last_kernel, n, dp),
         4,
@@ -557,16 +588,16 @@
         dmixed,
         qkv_full,
         dres_one,
-        qkv_part.astype(BF).reshape(dp, shard, 3 * local),
-        proj_part.astype(BF).reshape(dp, shard, local),
+        qkv_part.reshape(dp, shard, 3 * local),
+        proj_part.reshape(dp, shard, local),
         all_sums,
         biases,
     )
     qkv_out = qkv_turned.reshape(shard, 3, local).transpose(1, 0, 2)
     proj_out = proj_turned.T
     down_out = down_turned.T
-    qvbias_out = biases[0, : 2 * local].reshape(2, local)
-    upbias_out = biases[0, 2 * local :]
+    qvbias_out = jnp.stack([biases[0, :local], biases[0, 2 * local : 3 * local]])
+    upbias_out = biases[0, 3 * local :]
     pairs = all_sums.reshape(2, 3, width)
     gain_out, normbias_out, branch_out = pairs[:, 0], pairs[:, 1], pairs[:, 2]
     return (

time: 239 us -> 217 us (0.908)
  matrix products: 30.1 us -> 7.4 us
  Pallas kernels: 156 us -> 161 us
  local copies, waits for them, and re-layouts: 32.8 us -> 28.5 us
    dot_general x8 -> x1, matrix products: 23.1 us -> 0.66 us  [per_device(): mixed_rows = jnp.dot(rounded, qkv_full, preferred_element_type=F32)]
    pallas_call x0 -> x1, Pallas kernels: none -> 4.65 us  [per_device(): pl.pallas_call(attn_back_kernel, out_shape=[jax.ShapeDtypeStruct((total_r...]
    another operation x6 -> x0, local copies, waits for them, and re-layouts: 4.49 us -> none  [the longest x3 3.66 us: per_device(): jnp.stack([dquery, dkey, dvalue]).reshape(3, total_rows, local)]
    reshape x2 -> x3, local copies, waits for them, and re-layouts: 0.09 us -> 2.76 us  [the longest x2 2.76 us: per_device(): qkv_full = qkv_blocks.transpose(0, 2, 1, 3).reshape(width, 3 * local)]
    unnamed x89 -> x66, local copies, waits for them, and re-layouts: 17.7 us -> 17.9 us
  transfers between devices with their start and end apart: 2 -> 2, of which waited for: 0 -> 0; matrix products, arithmetic and copies ran while one was open for 4% -> 8% of each run, Pallas kernels for 24% -> 27%
where the time goes in v3:
time: 217 us; the launch traced here: 216 us
  Pallas kernels  161 us (74%)
  local copies, waits for them, and re-layouts  28.5 us (13%)
  between operations  15.2 us (7%)
  matrix products  7.4 us (3%)
  other arithmetic  2.54 us (1%)
    pallas_call x5, Pallas kernels, run(): pl.pallas_call(body, out_shape=[jax.ShapeDtypeStruct(shape, dtype) for sh...  157 us
    unnamed x66, local copies, waits for them, and re-layouts  17.9 us
    pallas_call x1, Pallas kernels, per_device(): pl.pallas_call(attn_back_kernel, out_shape=[jax.ShapeDtypeStruct((total_r...  4.65 us
  transfers between devices with their start and end apart: 2, of which 0 were waited for; matrix products, arithmetic and copies ran while one was open for 8% of the time, Pallas kernels for 27%

profile of v3, /device:TPU:0, one launch (start us, length us, event | category | flops | bytes accessed | tf_op | source)
XLA Modules:
  0.0 216.4 jit_solution(4721859300017896321)
XLA Ops:
  8.7 1.0 copy-done.4
  9.7 0.9 copy-done.15
  10.6 0.8 copy-done.18
  11.4 23.3 %shard_map.203 = (bf16[4,128,768]{2,1,0:T(8,128)(2,1)S(1)}, bf16[8,3,96,192]{3,2,1,0:T(8,128)(2,1)S(1)}, bf16[8,192,96]{2,1,0:T(8,128)(2,1)S(1)}) custom-call(f32[128,768]{1,0:T(8,128)S(1)} %copy-done.4, bf16[3,96,192]{2,1,0:T(8,128)(2,1)S(1)} %bitcast.95, bf16[192,96]{1,0:T(8,128)(2,1)S(1)} %bitcast.97), custom_call_target="tpu_custom_call" | custom-call | bytes 60000000 | tf_op jit(solution)/shard_map/pallas_call | solution.py:407
  34.7 1.7 copy.77
  36.5 2.1 reshape.125
  39.3 0.9 fusion.14
  40.9 1.2 copy.97
  42.1 2.0 copy.98
  44.1 1.1 add_convert_fusion
  46.2 0.8 copy.99.keyrow
  47.0 0.8 fusion
  48.5 0.9 fusion.9
  49.6 1.0 copy.85
  50.6 1.3 reshape.130.proj
  52.0 35.0 %shard_map.204 = (f32[128,768]{1,0:T(8,128)S(1)}, f32[128,1]{1,0:T(8,128)S(1)}, f32[128,768]{1,0:T(8,128)S(1)}, bf16[4,128,768]{2,1,0:T(8,128)(2,1)S(1)}) custom-call(bf16[512,192]{1,0:T(8,128)(2,1)S(1)} %copy.86.ctx, bf16[192,768]{1,0:T(8,128)(2,1)S(1)} %reshape.130.proj, f32[128,768]{1,0:T(8,128)S(1)} %copy-done.5, f32[1,768]{1,0:T(1,128)S(1)} %get-tuple-element.117.bias, ...), custom_call_target="tpu_custom_call" | custom-call | flops 150994944 | bytes 60000000 | tf_op jit(solution)/shard_map/pallas_call | solution.py:407
  87.8 0.7 copy-done.13
  89.2 0.9 copy-done.19
  90.0 1.6 copy.87
  91.7 2.4 %multiply_convert_fusion = (bf16[512,768]{1,0:T(8,128)(2,1)S(1)}, f32[512,768]{1,0:T(8,128)S(1)}) fusion(f32[768]{0:T(1024)S(1)} %reduce.4, bf16[512,768]{1,0:T(8,128)(2,1)} %bitcast.98, bf16[1,768,768]{2,1,0:T(8,128)(2,1)} %all-gather.5.cloned.1.call-done), kind=kOutput, calls=%fused_computation.10 | convolution fusion | flops 606339072 | bytes 4328448 | tf_op jit(solution)/shard_map/dot_general | solution.py:505
  94.1 31.7 %shard_map.205 = (f32[128,768]{1,0:T(8,128)S(1)}, f32[128,768]{1,0:T(8,128)S(1)}, f32[3,768]{1,0:T(4,128)S(1)}, bf16[4,128,768]{2,1,0:T(8,128)(2,1)S(1)}) custom-call(bf16[512,768]{1,0:T(8,128)(2,1)S(1)} %get-tuple-element.124.act, bf16[768,768]{1,0:T(8,128)(2,1)S(1)} %bitcast.82, f32[128,768]{1,0:T(8,128)S(1)} %copy-done.10, ...), custom_call_target="tpu_custom_call" | custom-call | flops 603979776 | bytes 60000000 | tf_op jit(solution)/shard_map/pallas_call | solution.py:407
  125.9 0.7 copy-done.11
  126.6 0.8 convolution_convert_fusion
  127.9 1.1 fusion.13
  129.0 0.8 convolution_convert_fusion.1
  130.4 42.8 %shard_map.206 = (f32[128,768]{1,0:T(8,128)S(1)}, f32[3,768]{1,0:T(4,128)S(1)}, bf16[4,128,768]{2,1,0:T(8,128)(2,1)S(1)}, f32[96,768]{1,0:T(8,128)S(1)}, f32[96,768]{1,0:T(8,128)S(1)}) custom-call(bf16[512,768]{1,0:T(8,128)(2,1)S(1)} %get-tuple-element.106.dpre, bf16[768,768]{1,0:T(8,128)(2,1)S(1)} %bitcast.86, f32[128,768]{1,0:T(8,128)S(1)} %get-tuple-element.43.dres_two, ...), custom_call_target="tpu_custom_call" | custom-call | flops 603979776 | bytes 60000000 | tf_op jit(solution)/shard_map/pallas_call | solution.py:407
  173.2 4.6 %shard_map.207 = (bf16[512,576]{1,0:T(8,128)(2,1)S(1)}, bf16[768,576]{1,0:T(8,128)(2,1)S(1)}, bf16[768,192]{1,0:T(8,128)(2,1)S(1)}, f32[1,576]{1,0:T(1,128)S(1)}) custom-call(s32[1]{0:T(128)} %copy.104.lengths, bf16[512,768]{1,0:T(8,128)(2,1)S(1)} %bitcast.90, bf16[192,768]{1,0:T(8,128)(2,1)S(1)} %reshape.130.proj, bf16[512,192]{1,0:T(8,128)(2,1)S(1)} %copy.86.ctx, ...), custom_call_target="tpu_custom_call" | custom-call | tf_op jit(solution)/shard_map/pallas_call | solution.py:551
  177.9 23.8 %shard_map.208 = (f32[128,768]{1,0:T(8,128)S(1)}, f32[96,576]{1,0:T(8,128)S(1)}, f32[96,192]{1,0:T(8,128)S(1)}, f32[6,768]{1,0:T(8,128)S(1)}, f32[1,1344]{1,0:T(1,128)S(1)}) custom-call(bf16[512,576]{1,0:T(8,128)(2,1)S(1)} %get-tuple-element.47.dmix, bf16[768,576]{1,0:T(8,128)(2,1)S(1)} %copy.89.qkv, f32[128,768]{1,0:T(8,128)S(1)} %get-tuple-element.48.dres, ...), custom_call_target="tpu_custom_call" | custom-call | flops 452984832 | bytes 60000000 | tf_op jit(solution)/shard_map/pallas_call | solution.py:407
  202.6 0.9 copy.91
  203.5 0.7 copy.92
  206.6 0.7 copy.105
  207.4 0.7 copy.106
  (81 shorter events, 11.2 us)
Async XLA Ops:
  7.2 82.9 %all-gather.7.cloned.1.call-start = ((), (), s32[]{:S(2)}) async-start(), calls=%async_computation.1 | async-start | bytes 1327104 | tf_op jit(solution)/shard_map/all_gather | solution.py:460
  7.9 83.7 %all-gather.5.cloned.1.call-start = ((), (), s32[]{:S(2)}) async-start(), calls=%async_computation | async-start | bytes 1327104 | tf_op jit(solution)/shard_map/all_gather | solution.py:459
  8.7 1.0 copy-start.4
  9.7 0.9 copy-start.15
  10.6 0.8 copy-start.18
  38.6 1.6 copy-start.26
  45.2 2.6 %copy-start = (bf16[512,192]{1,0:T(8,128)(2,1)}, bf16[512,192]{1,0:T(8,128)(2,1)S(1)}, u32[]{:S(2)}) copy-start(bf16[512,192]{1,0:T(8,128)(2,1)S(1)} %get-tuple-element.129.query) | copy-start | bytes 589828
  45.2 2.6 %copy-start.2 = (bf16[512,192]{1,0:T(8,128)(2,1)}, bf16[512,192]{1,0:T(8,128)(2,1)S(1)}, u32[]{:S(2)}) copy-start(bf16[512,192]{1,0:T(8,128)(2,1)S(1)} %get-tuple-element.130.value) | copy-start | bytes 589828
  49.4 2.6 %copy-start.25 = (f32[1,768]{1,0:T(1,128)S(1)}, f32[1,768]{1,0:T(1,128)}, u32[]{:S(2)}) copy-start(f32[1,768]{1,0:T(1,128)} %param.19) | copy-start | bytes 9220
  49.4 2.6 %copy-start.22 = (f32[1,2,768]{2,1,0:T(2,128)S(1)}, f32[1,2,768]{2,1,0:T(2,128)}, u32[]{:S(2)}) copy-start(f32[1,2,768]{2,1,0:T(2,128)} %param.17) | copy-start | bytes 18436
  49.4 2.6 %copy-start.23 = (f32[1,2,768]{2,1,0:T(2,128)S(1)}, f32[1,2,768]{2,1,0:T(2,128)}, u32[]{:S(2)}) copy-start(f32[1,2,768]{2,1,0:T(2,128)} %param.22) | copy-start | bytes 18436
  49.4 2.6 %copy-start.24 = (f32[1,2,768]{2,1,0:T(2,128)S(1)}, f32[1,2,768]{2,1,0:T(2,128)}, u32[]{:S(2)}) copy-start(f32[1,2,768]{2,1,0:T(2,128)} %param.21) | copy-start | bytes 18436
  49.4 2.6 %copy-start.5 = (f32[128,768]{1,0:T(8,128)S(1)}, f32[128,768]{1,0:T(8,128)}, u32[]{:S(2)}) copy-start(f32[128,768]{1,0:T(8,128)} %hidden.1) | copy-start | bytes 1179652
  87.0 0.7 copy-start.9
  87.8 0.7 copy-start.13
  88.5 0.6 copy-start.16
  89.1 0.9 copy-start.19
  91.6 2.5 %copy-start.8 = (f32[128,768]{1,0:T(8,128)S(1)}, f32[128,768]{1,0:T(8,128)}, u32[]{:S(2)}) copy-start(f32[128,768]{1,0:T(8,128)} %cot.1) | copy-start | bytes 1179652
  91.6 2.5 %copy-start.10 = (f32[128,768]{1,0:T(8,128)S(1)}, f32[128,768]{1,0:T(8,128)}, u32[]{:S(2)}) copy-start(f32[128,768]{1,0:T(8,128)} %copy-done.9) | copy-start | bytes 1179652
  125.9 0.7 copy-start.11
  126.6 1.3 copy-start.21
  127.9 1.1 copy-start.20
  129.0 1.3 copy-start.6
  129.0 1.3 copy-start.14
  129.0 1.3 copy-start.17
  130.4 42.8 %copy-start.1 = (bf16[512,192]{1,0:T(8,128)(2,1)S(1)}, bf16[512,192]{1,0:T(8,128)(2,1)}, u32[]{:S(2)}) copy-start(bf16[512,192]{1,0:T(8,128)(2,1)} %copy-done) | copy-start | bytes 589828
  130.4 42.8 %copy-start.3 = (bf16[512,192]{1,0:T(8,128)(2,1)S(1)}, bf16[512,192]{1,0:T(8,128)(2,1)}, u32[]{:S(2)}) copy-start(bf16[512,192]{1,0:T(8,128)(2,1)} %copy-done.2) | copy-start | bytes 589828
  130.4 42.8 %copy-start.7 = (bf16[512,192]{1,0:T(8,128)(2,1)S(1)}, bf16[512,192]{1,0:T(8,128)(2,1)}, u32[]{:S(2)}) copy-start(bf16[512,192]{1,0:T(8,128)(2,1)} %copy.99.keyrow) | copy-start | bytes 589828
  201.8 4.9 %copy-start.12 = (f32[128,768]{1,0:T(8,128)S(1)}, f32[128,768]{1,0:T(8,128)}, u32[]{:S(2)}) copy-start(f32[128,768]{1,0:T(8,128)} %copy-done.11) | copy-start | bytes 1179652
Sparse Core Ops, SparseCore 0:
  9.9 31.2 all-gather.6
  43.0 24.0 all-gather.4

commit v4 on v3

--- a/solution.py
+++ b/solution.py
@@ -45,13 +45,6 @@
         0.5 * (1.0 + lax.erf(pre_act * half_root))
         + pre_act * jnp.exp(-0.5 * pre_act * pre_act) * inv_root
     )
-
-
-def score_block(queries, key_rows, key_valid):
-    raw_scores = jnp.einsum(
-        "sqhc,skhc->shqk", queries, key_rows, preferred_element_type=jnp.float32
-    ) * (1.0 / math.sqrt(HD))
-    return jnp.where(key_valid[:, None, None, :], raw_scores, -1e30)
 
 
 def send(src, dst, send_sem, recv_sem, axis, target):
@@ -332,6 +325,35 @@
 
 def tn_dot(left, right):
     return lax.dot_general(left, right, (((0,), (0,)), ((), ())), preferred_element_type=F32)
+
+
+def attn_kernel(
+    lengths, rounded, qkv_all, proj_all, bias,
+    query, keyrow, value, ctx, qkv_o, proj_o,
+):
+    dp, local, shard = proj_all.shape
+    scale = 1.0 / math.sqrt(HD)
+    for d in range(dp):
+        part = slice(d * shard, (d + 1) * shard)
+        for j in range(3):
+            qkv_o[part, j * local : (j + 1) * local] = qkv_all[d, j]
+        proj_o[:, part] = proj_all[d]
+    mixed = jnp.dot(rounded[...], qkv_o[...], preferred_element_type=F32)
+    query[...] = (mixed[:, :local] + bias[0:1, :]).astype(BF)
+    keyrow[...] = mixed[:, local : 2 * local].astype(BF)
+    value[...] = (mixed[:, 2 * local :] + bias[1:2, :]).astype(BF)
+    for seq in range(ctx.shape[0] // L):
+        rows = slice(seq * L, (seq + 1) * L)
+        valid = lax.broadcasted_iota(jnp.int32, (L, L), 1) < lengths[seq]
+        for head in range(local // HD):
+            cols = slice(head * HD, (head + 1) * HD)
+            scores = nt_dot(query[rows, cols], keyrow[rows, cols]) * scale
+            scores = jnp.where(valid, scores, -1e30)
+            weights = jnp.exp(scores - jnp.max(scores, axis=-1, keepdims=True))
+            prob = weights * (1.0 / jnp.sum(weights, axis=-1, keepdims=True))
+            ctx[rows, cols] = jnp.dot(
+                prob.astype(BF), value[rows, cols], preferred_element_type=F32
+            ).astype(BF)
 
 
 def attn_back_kernel(
@@ -447,11 +469,7 @@
     n = lax.axis_size("tensor")
     dp = lax.axis_size("dp")
     own_rows, width = inputs.shape
-    seq_count = lengths.shape[0]
     local = qkv_weight.shape[3]
-    head_count = local // HD
-    head_shape = (seq_count, L, head_count, HD)
-    key_valid = jnp.arange(L, dtype=jnp.int32)[None, :] < lengths[:, None]
     total_rows = own_rows * n
     own = (own_rows, width)
     spread = ((n, own_rows, width), BF)
@@ -470,24 +488,19 @@
         proj_weight[0],
     )
     rounded = rounded.reshape(total_rows, width)
-    qkv_full = qkv_blocks.transpose(0, 2, 1, 3).reshape(width, 3 * local)
-    proj_full = proj_blocks.transpose(1, 0, 2).reshape(local, width)
-    mixed_rows = jnp.dot(rounded, qkv_full, preferred_element_type=F32)
-    queries_2d = (mixed_rows[:, :local] + qv_bias[0, 0]).astype(BF)
-    key_2d = mixed_rows[:, local : 2 * local].astype(BF)
-    values_2d = (mixed_rows[:, 2 * local :] + qv_bias[0, 1]).astype(BF)
-    queries = queries_2d.reshape(head_shape)
-    key_rows = key_2d.reshape(head_shape)
-    values = values_2d.reshape(head_shape)
-    scores = score_block(queries, key_rows, key_valid)
-    row_peak = jnp.max(scores, axis=-1, keepdims=True)
-    log_total = row_peak + jnp.log(jnp.sum(jnp.exp(scores - row_peak), axis=-1, keepdims=True))
-    soft_weights = jnp.exp(scores - log_total).astype(BF)
-    context = (
-        jnp.einsum("shqk,skhc->sqhc", soft_weights, values, preferred_element_type=F32)
-        .astype(BF)
-        .reshape(total_rows, local)
-    )
+    vmem = pl.BlockSpec(memory_space=pltpu.VMEM)
+    heads = jax.ShapeDtypeStruct((total_rows, local), BF)
+    queries_2d, key_2d, values_2d, context, qkv_full, proj_full = pl.pallas_call(
+        attn_kernel,
+        out_shape=[heads] * 4
+        + [
+            jax.ShapeDtypeStruct((width, 3 * local), BF),
+            jax.ShapeDtypeStruct((local, width), BF),
+        ],
+        in_specs=[pl.BlockSpec(memory_space=pltpu.SMEM)] + [vmem] * 4,
+        out_specs=[vmem] * 6,
+        compiler_params=pltpu.CompilerParams(vmem_limit_bytes=40 * 2**20),
+    )(lengths, rounded, qkv_blocks, proj_blocks, qv_bias[0])
     normed_one, inverse_one, middle, middle_rows = run(
         functools.partial(attn_out_kernel, n),
         1,
@@ -547,7 +560,6 @@
         down_part.astype(BF).reshape(dp, shard, units),
     )
     dres_one_all = dres_one_all.reshape(total_rows, width)
-    vmem = pl.BlockSpec(memory_space=pltpu.VMEM)
     dmixed, qkv_part, proj_part, mix_sums = pl.pallas_call(
         attn_back_kernel,
         out_shape=[

time: 217 us -> 204 us (0.940)
  local copies, waits for them, and re-layouts: 28.5 us -> 18.5 us
  matrix products: 7.4 us -> 5.14 us
    reshape x4 -> x0, local copies, waits for them, and re-layouts: 4.23 us -> none  [the longest x2 2.76 us: per_device(): qkv_full = qkv_blocks.transpose(0, 2, 1, 3).reshape(width, 3 * local)]
    transpose x2 -> x0, local copies, waits for them, and re-layouts: 2.75 us -> none  [the longest x1 1.75 us: per_device(): qkv_full = qkv_blocks.transpose(0, 2, 1, 3).reshape(width, 3 * local)]
    pallas_call x0 -> x1, Pallas kernels: none -> 2.52 us  [per_device(): pl.pallas_call(attn_kernel, out_shape=[heads] * 4 + [jax.ShapeDtypeStruct...]
    dot_general x3 -> x0, matrix products: 2.28 us -> none  [the longest x1 0.85 us: per_device(): jnp.einsum('shqk,skhc->sqhc', soft_weights, values, preferred_element_typ...]
    unnamed x66 -> x69, local copies, waits for them, and re-layouts: 17.9 us -> 16 us
  transfers between devices with their start and end apart: 2 -> 2, of which waited for: 0 -> 0; matrix products, arithmetic and copies ran while one was open for 8% -> 1% of each run, Pallas kernels for 27% -> 30%
where the time goes in v4:
time: 204 us
  Pallas kernels  162 us (79%)
  local copies, waits for them, and re-layouts  18.5 us (9%)
  between operations  15.1 us (7%)
  matrix products  5.14 us (3%)
    pallas_call x5, Pallas kernels, run(): pl.pallas_call(body, out_shape=[jax.ShapeDtypeStruct(shape, dtype) for sh...  155 us
    unnamed x69, local copies, waits for them, and re-layouts  16 us
    pallas_call x1, Pallas kernels, per_device(): pl.pallas_call(attn_back_kernel, out_shape=[jax.ShapeDtypeStruct((total_r...  4.7 us
  transfers between devices with their start and end apart: 2, of which 0 were waited for; matrix products, arithmetic and copies ran while one was open for 1% of the time, Pallas kernels for 30%

profile of v4, /device:TPU:0, one launch (start us, length us, event | category | flops | bytes accessed | tf_op | source)
XLA Modules:
  0.0 203.6 jit_solution(14019917927409303054)
XLA Ops:
  7.2 0.7 all-gather.7.cloned.1.call-update
  8.0 0.7 all-gather.5.cloned.1.call-update
  9.3 0.7 reduce
  10.1 1.0 copy-done
  11.0 0.9 copy-done.19
  12.0 0.8 copy-done.22
  12.7 23.4 %shard_map.203 = (bf16[4,128,768]{2,1,0:T(8,128)(2,1)S(1)}, bf16[8,3,96,192]{3,2,1,0:T(8,128)(2,1)S(1)}, bf16[8,192,96]{2,1,0:T(8,128)(2,1)S(1)}) custom-call(f32[128,768]{1,0:T(8,128)S(1)} %copy-done, bf16[3,96,192]{2,1,0:T(8,128)(2,1)S(1)} %bitcast.71, bf16[192,96]{1,0:T(8,128)(2,1)S(1)} %bitcast.73), custom_call_target="tpu_custom_call" | custom-call | bytes 60000000 | tf_op jit(solution)/shard_map/pallas_call | solution.py:429
  36.2 0.7 copy-done.23
  36.9 2.5 %shard_map.204 = (bf16[512,192]{1,0:T(8,128)(2,1)S(1)}, bf16[512,192]{1,0:T(8,128)(2,1)S(1)}, bf16[512,192]{1,0:T(8,128)(2,1)S(1)}, bf16[512,192]{1,0:T(8,128)(2...) custom-call(s32[1]{0:T(128)S(6)} %copy.47.lengths, bf16[512,768]{1,0:T(8,128)(2,1)S(1)} %bitcast.61, ...), custom_call_target="tpu_custom_call" | custom-call | tf_op jit(solution)/shard_map/pallas_call | solution.py:493
  39.4 0.7 copy-done.13
  40.1 0.7 copy-done.15
  40.8 0.7 copy-done.17
  41.6 34.8 %shard_map.205 = (f32[128,768]{1,0:T(8,128)S(1)}, f32[128,1]{1,0:T(8,128)S(1)}, f32[128,768]{1,0:T(8,128)S(1)}, bf16[4,128,768]{2,1,0:T(8,128)(2,1)S(1)}) custom-call(bf16[512,192]{1,0:T(8,128)(2,1)S(1)} %get-tuple-element.45.ctx, bf16[192,768]{1,0:T(8,128)(2,1)S(1)} %get-tuple-element.46.proj, f32[128,768]{1,0:T(8,128)S(1)} %copy-done, ...), custom_call_target="tpu_custom_call" | custom-call | flops 150994944 | bytes 60000000 | tf_op jit(solution)/shard_map/pallas_call | solution.py:429
  76.3 0.7 copy-done.3
  77.1 0.7 copy-done.7
  78.5 0.9 copy-done.24
  79.4 1.6 copy.36
  81.0 2.4 %multiply_convert_fusion = (bf16[512,768]{1,0:T(8,128)(2,1)S(1)}, f32[512,768]{1,0:T(8,128)S(1)}) fusion(f32[768]{0:T(1024)S(1)} %reduce, bf16[512,768]{1,0:T(8,128)(2,1)} %bitcast.75, bf16[1,768,768]{2,1,0:T(8,128)(2,1)} %all-gather.5.cloned.1.call-done), kind=kOutput, calls=%fused_computation.6 | convolution fusion | flops 606339072 | bytes 4328448 | tf_op jit(solution)/shard_map/dot_general | solution.py:518
  83.5 31.9 %shard_map.206 = (f32[128,768]{1,0:T(8,128)S(1)}, f32[128,768]{1,0:T(8,128)S(1)}, f32[3,768]{1,0:T(4,128)S(1)}, bf16[4,128,768]{2,1,0:T(8,128)(2,1)S(1)}) custom-call(bf16[512,768]{1,0:T(8,128)(2,1)S(1)} %get-tuple-element.119.act, bf16[768,768]{1,0:T(8,128)(2,1)S(1)} %bitcast.60, f32[128,768]{1,0:T(8,128)S(1)} %copy-done.4, ...), custom_call_target="tpu_custom_call" | custom-call | flops 603979776 | bytes 60000000 | tf_op jit(solution)/shard_map/pallas_call | solution.py:429
  115.4 0.8 convolution_convert_fusion
  116.8 1.1 fusion.7
  117.9 0.8 convolution_convert_fusion.1
  119.3 40.9 %shard_map.207 = (f32[128,768]{1,0:T(8,128)S(1)}, f32[3,768]{1,0:T(4,128)S(1)}, bf16[4,128,768]{2,1,0:T(8,128)(2,1)S(1)}, f32[96,768]{1,0:T(8,128)S(1)}, f32[96,768]{1,0:T(8,128)S(1)}) custom-call(bf16[512,768]{1,0:T(8,128)(2,1)S(1)} %get-tuple-element.107.dpre, bf16[768,768]{1,0:T(8,128)(2,1)S(1)} %bitcast.63, f32[128,768]{1,0:T(8,128)S(1)} %get-tuple-element.51.dres_two, ...), custom_call_target="tpu_custom_call" | custom-call | flops 603979776 | bytes 60000000 | tf_op jit(solution)/shard_map/pallas_call | solution.py:429
  160.3 4.7 %shard_map.208 = (bf16[512,576]{1,0:T(8,128)(2,1)S(1)}, bf16[768,576]{1,0:T(8,128)(2,1)S(1)}, bf16[768,192]{1,0:T(8,128)(2,1)S(1)}, f32[1,576]{1,0:T(1,128)S(1)}) custom-call(s32[1]{0:T(128)S(6)} %copy.47.lengths, bf16[512,768]{1,0:T(8,128)(2,1)S(1)} %bitcast.67, bf16[192,768]{1,0:T(8,128)(2,1)S(1)} %get-tuple-element.46.proj, ...), custom_call_target="tpu_custom_call" | custom-call | tf_op jit(solution)/shard_map/pallas_call | solution.py:563
  165.1 23.9 %shard_map.209 = (f32[128,768]{1,0:T(8,128)S(1)}, f32[96,576]{1,0:T(8,128)S(1)}, f32[96,192]{1,0:T(8,128)S(1)}, f32[6,768]{1,0:T(8,128)S(1)}, f32[1,1344]{1,0:T(1,128)S(1)}) custom-call(bf16[512,576]{1,0:T(8,128)(2,1)S(1)} %get-tuple-element.58.dmix, bf16[768,576]{1,0:T(8,128)(2,1)S(1)} %get-tuple-element.59.qkv, f32[128,768]{1,0:T(8,128)S(1)} %get-tuple-element.60.dres, ...), custom_call_target="tpu_custom_call" | custom-call | flops 452984832 | bytes 60000000 | tf_op jit(solution)/shard_map/pallas_call | solution.py:429
  189.0 0.7 slice.46
  191.5 0.7 copy.39
  192.4 0.9 copy.38
  193.9 0.7 copy.48
  194.6 0.7 copy.49
  195.4 0.7 copy.50
  196.1 0.7 copy.51
  (67 shorter events, 4.6 us)
Async XLA Ops:
  7.2 72.2 %all-gather.7.cloned.1.call-start = ((), (), s32[]{:S(2)}) async-start(), calls=%async_computation.1 | async-start | bytes 1327104 | tf_op jit(solution)/shard_map/all_gather | solution.py:478
  7.9 33.6 %copy-start.27 = (f32[1,2,768]{2,1,0:T(2,128)S(1)}, f32[1,2,768]{2,1,0:T(2,128)}, u32[]{:S(2)}) copy-start(f32[1,2,768]{2,1,0:T(2,128)} %param.17) | copy-start | bytes 18436
  7.9 33.6 %copy-start.28 = (f32[1,2,768]{2,1,0:T(2,128)S(1)}, f32[1,2,768]{2,1,0:T(2,128)}, u32[]{:S(2)}) copy-start(f32[1,2,768]{2,1,0:T(2,128)} %param.22) | copy-start | bytes 18436
  7.9 33.6 %copy-start.29 = (f32[1,2,768]{2,1,0:T(2,128)S(1)}, f32[1,2,768]{2,1,0:T(2,128)}, u32[]{:S(2)}) copy-start(f32[1,2,768]{2,1,0:T(2,128)} %param.21) | copy-start | bytes 18436
  7.9 73.0 %all-gather.5.cloned.1.call-start = ((), (), s32[]{:S(2)}) async-start(), calls=%async_computation | async-start | bytes 1327104 | tf_op jit(solution)/shard_map/all_gather | solution.py:477
  10.0 1.0 copy-start
  11.0 0.9 copy-start.19
  11.9 0.8 copy-start.22
  36.2 0.7 copy-start.23
  39.4 0.7 copy-start.13
  40.1 0.7 copy-start.15
  40.8 0.7 copy-start.17
  76.3 0.7 copy-start.3
  77.1 0.7 copy-start.7
  77.8 0.6 copy-start.20
  78.5 0.9 copy-start.24
  81.0 2.5 %copy-start.2 = (f32[128,768]{1,0:T(8,128)S(1)}, f32[128,768]{1,0:T(8,128)}, u32[]{:S(2)}) copy-start(f32[128,768]{1,0:T(8,128)} %cot.1) | copy-start | bytes 1179652
  81.0 2.5 %copy-start.4 = (f32[128,768]{1,0:T(8,128)S(1)}, f32[128,768]{1,0:T(8,128)}, u32[]{:S(2)}) copy-start(f32[128,768]{1,0:T(8,128)} %copy-done.3) | copy-start | bytes 1179652
  115.3 0.8 copy-start.5
  115.4 1.4 copy-start.26
  116.8 1.1 copy-start.25
  117.9 1.3 copy-start.1
  117.9 1.3 copy-start.8
  117.9 1.3 copy-start.21
  119.3 41.0 %copy-start.14 = (bf16[512,192]{1,0:T(8,128)(2,1)S(1)}, bf16[512,192]{1,0:T(8,128)(2,1)}, u32[]{:S(2)}) copy-start(bf16[512,192]{1,0:T(8,128)(2,1)} %copy-done.13) | copy-start | bytes 589828
  119.3 41.0 %copy-start.16 = (bf16[512,192]{1,0:T(8,128)(2,1)S(1)}, bf16[512,192]{1,0:T(8,128)(2,1)}, u32[]{:S(2)}) copy-start(bf16[512,192]{1,0:T(8,128)(2,1)} %copy-done.15) | copy-start | bytes 589828
  119.3 41.0 %copy-start.18 = (bf16[512,192]{1,0:T(8,128)(2,1)S(1)}, bf16[512,192]{1,0:T(8,128)(2,1)}, u32[]{:S(2)}) copy-start(bf16[512,192]{1,0:T(8,128)(2,1)} %copy-done.17) | copy-start | bytes 589828
  160.2 28.8 %copy-start.9 = (f32[96,768]{1,0:T(8,128)}, f32[96,768]{1,0:T(8,128)S(1)}, u32[]{:S(2)}) copy-start(f32[96,768]{1,0:T(8,128)S(1)} %get-tuple-element.72) | copy-start | bytes 884740
  160.2 28.8 %copy-start.11 = (f32[96,768]{1,0:T(8,128)}, f32[96,768]{1,0:T(8,128)S(1)}, u32[]{:S(2)}) copy-start(f32[96,768]{1,0:T(8,128)S(1)} %get-tuple-element.71) | copy-start | bytes 884740
  189.0 4.9 %copy-start.6 = (f32[128,768]{1,0:T(8,128)S(1)}, f32[128,768]{1,0:T(8,128)}, u32[]{:S(2)}) copy-start(f32[128,768]{1,0:T(8,128)} %copy-done.5) | copy-start | bytes 1179652
  189.0 6.4 %copy-start.12 = (f32[96,768]{1,0:T(8,128)S(1)}, f32[96,768]{1,0:T(8,128)}, u32[]{:S(2)}) copy-start(f32[96,768]{1,0:T(8,128)} %copy-done.11) | copy-start | bytes 884740
  192.3 3.8 %copy-start.10 = (f32[96,768]{1,0:T(8,128)S(1)}, f32[96,768]{1,0:T(8,128)}, u32[]{:S(2)}) copy-start(f32[96,768]{1,0:T(8,128)} %copy-done.9) | copy-start | bytes 884740
Sparse Core Ops, SparseCore 0:
  9.9 32.5 all-gather.6
  44.4 24.0 all-gather.4
